TPU v7x, 512 devices: a whole 4x4x16 slice. The times are simulated.
512 devices in a mesh: seq: 64 (over z_hi, x, y, core), head: 8 (over z_lo).
Axes of the slice: x: 4, y: 4, z: 16 (z_hi: 2, z_lo: 8; z = z_hi * 8 + z_lo), core: 2. Of those that a mesh axis runs over, the one named last changes fastest.
Arguments:
- queries: bfloat16 [16384, 2048], P('seq', 'head'), may hold values from -6 to 6
- keys: bfloat16 [16384, 2048], P('seq', 'head'), may hold values from -6 to 6
- values: bfloat16 [16384, 2048], P('seq', 'head'), may hold values from -6 to 6
- partner: int32 [16, 64], P('head'), may hold values from 0 to 63, each once within a row
Outputs:
- attended: bfloat16 [16384, 2048], P('seq', 'head')
Inputs may be any that keep to these rules, and one draw needn't show every extreme that they name: `partner`: each row is a permutation of the 64 block indices.
All inputs are finite; a program needn't handle non-finite values.
Results may differ from a plain program's by a relative error of at most 0.0049.
Values may be sent and summed in bfloat16 or wider, within the bound.
A program may use at most 64 MiB of HBM per device.

v0:
```python
import math

import jax
import jax.numpy as jnp
from jax import lax
from jax.sharding import PartitionSpec as P

HEADS = 16
DH = 128
BS = 256
SINK_ITERS = 8


sharpness = 2.0


def side_by_side(arrays, axis, split_dim, concat_dim, along):
    both = jnp.concatenate(arrays, axis=along)
    whole, at, finished = (
        lax.all_to_all(both, axis, split_axis=split_dim, concat_axis=concat_dim, tiled=True),
        0,
        [],
    )
    for a in arrays:
        finished.append(lax.slice_in_dim(whole, at, at + a.shape[along], axis=along))
        at += a.shape[along]
    return tuple(finished)


def shortened(value):

    def short(part):
        return part.astype(jnp.bfloat16) if part.dtype == jnp.float32 else part

    return jax.tree.map(short, value)


def shifted(block, axis, distance):
    devices = range(lax.axis_size(axis))
    route = [(i - distance, i) for i in devices if i - distance in devices]
    return lax.ppermute(block, axis, route)


def from_everyone(value, axis):
    copies = jnp.broadcast_to(value, (lax.axis_size(axis), *value.shape))
    return lax.all_to_all(copies, axis, split_axis=0, concat_axis=0, tiled=True)


def laid_out(parts, dim):
    dims = list(parts.shape[1:])
    dims[dim] *= parts.shape[0]
    return jnp.moveaxis(parts, 0, dim).reshape(dims)


def gathered_copies(value, axis, dim):
    parts = from_everyone(value, axis)
    return laid_out(parts, dim)


def taken_together(value, axis):
    everything = from_everyone(value, axis)
    return jnp.sum(everything, axis=0)


def log_sum(values_in, along):
    col_top = jnp.max(values_in, axis=along, keepdims=True)
    return col_top + jnp.log(jnp.sum(jnp.exp(values_in - col_top), axis=along, keepdims=True))


def fetch_partners(key_blocks, value_blocks, partner, seq_count):
    blocks, block_len, feat_width = key_blocks.shape
    all_blocks = blocks * seq_count
    heads_here = feat_width // DH
    piece_rows = block_len // seq_count
    spread = side_by_side(
        (
            key_blocks.reshape(blocks, seq_count, piece_rows, feat_width),
            value_blocks.reshape(blocks, seq_count, piece_rows, feat_width),
        ),
        "seq",
        1,
        0,
        2,
    )
    held_pair = tuple((part.reshape(all_blocks, piece_rows, feat_width) for part in spread))
    picked = tuple(
        (
            jnp.concatenate(
                [
                    jnp.take(
                        held[:, :, head_index * DH : (head_index + 1) * DH],
                        partner[head_index],
                        axis=0,
                    )
                    for head_index in range(heads_here)
                ],
                axis=2,
            )
            for held in held_pair
        )
    )
    picked = tuple((part.reshape(seq_count, blocks, piece_rows, feat_width) for part in picked))
    returned = jax.tree.map(
        lambda part, own: part.astype(own.dtype),
        lax.all_to_all(shortened(picked), "seq", split_axis=0, concat_axis=2, tiled=True),
        picked,
    )
    return tuple((part.reshape(blocks, block_len, feat_width) for part in returned))


def body(queries, keys, values, partner):
    seq_count = lax.axis_size("seq")
    position = lax.axis_index("seq")
    row_count, feat_width = queries.shape
    blocks = row_count // BS
    all_blocks = blocks * seq_count
    heads_here = feat_width // DH
    query_blocks = queries.reshape(blocks, BS, feat_width)
    key_blocks = keys.reshape(blocks, BS, feat_width)
    value_blocks = values.reshape(blocks, BS, feat_width)
    last_key, last_value = shifted((key_blocks[-1], value_blocks[-1]), "seq", 1)
    key_prev = jnp.concatenate([last_key[None], key_blocks[:-1]], axis=0)
    value_prev = jnp.concatenate([last_value[None], value_blocks[:-1]], axis=0)
    pooled_q = jnp.sum(query_blocks, axis=1, dtype=jnp.float32) / math.sqrt(BS)
    pooled_k = jnp.sum(key_blocks, axis=1, dtype=jnp.float32) / math.sqrt(BS)
    every_key = gathered_copies(pooled_k, "seq", 0)
    partial_value = jnp.dot(
        pooled_q, every_key.T, precision=lax.Precision.HIGHEST, preferred_element_type=jnp.float32
    ) * (sharpness / math.sqrt(HEADS * DH))
    scores = taken_together(partial_value, "head")
    log_plan = gathered_copies(scores, "seq", 0)
    for sweep in range(SINK_ITERS):
        log_plan = log_plan - log_sum(log_plan, 1)
        log_plan = log_plan - log_sum(log_plan, 0)
    log_plan = lax.dynamic_slice_in_dim(log_plan, position * blocks, blocks, 0)
    own_partner = lax.dynamic_slice_in_dim(partner, position * blocks, blocks, 1)
    partner_bias = math.log(all_blocks) + jnp.take_along_axis(
        log_plan, jnp.transpose(own_partner), axis=1
    )
    key_part, value_part = fetch_partners(key_blocks, value_blocks, partner, seq_count)
    keep_prev = position * blocks + jnp.arange(blocks, dtype=jnp.int32) > 0
    inv_scale = 1.0 / math.sqrt(DH)
    outputs = []
    for head_index in range(heads_here):
        low = head_index * DH
        high = low + DH
        query_head = query_blocks[:, :, low:high]
        logit_prev = (
            jnp.einsum(
                "gqd,gkd->gqk",
                query_head,
                key_prev[:, :, low:high],
                preferred_element_type=jnp.float32,
            )
            * inv_scale
        )
        logit_prev = jnp.where(keep_prev[:, None, None], logit_prev, -jnp.inf)
        logit_local = (
            jnp.einsum(
                "gqd,gkd->gqk",
                query_head,
                key_blocks[:, :, low:high],
                preferred_element_type=jnp.float32,
            )
            * inv_scale
        )
        logit_part = (
            jnp.einsum(
                "gqd,gkd->gqk",
                query_head,
                key_part[:, :, low:high],
                preferred_element_type=jnp.float32,
            )
            * inv_scale
            + partner_bias[:, head_index][:, None, None]
        )
        row_top = jnp.maximum(
            jnp.maximum(
                jnp.max(logit_prev, axis=2, keepdims=True),
                jnp.max(logit_local, axis=2, keepdims=True),
            ),
            jnp.max(logit_part, axis=2, keepdims=True),
        )
        expo_prev = jnp.exp(logit_prev - row_top)
        expo_local = jnp.exp(logit_local - row_top)
        expo_part = jnp.exp(logit_part - row_top)
        denom = (
            jnp.sum(expo_prev, axis=2, keepdims=True)
            + jnp.sum(expo_local, axis=2, keepdims=True)
            + jnp.sum(expo_part, axis=2, keepdims=True)
        )
        weight_prev = (expo_prev / denom).astype(jnp.bfloat16)
        weight_local = (expo_local / denom).astype(jnp.bfloat16)
        weight_part = (expo_part / denom).astype(jnp.bfloat16)
        mixed = jnp.einsum(
            "gqk,gkd->gqd",
            weight_prev,
            value_prev[:, :, low:high],
            preferred_element_type=jnp.float32,
        )
        mixed = mixed + jnp.einsum(
            "gqk,gkd->gqd",
            weight_local,
            value_blocks[:, :, low:high],
            preferred_element_type=jnp.float32,
        )
        mixed = mixed + jnp.einsum(
            "gqk,gkd->gqd",
            weight_part,
            value_part[:, :, low:high],
            preferred_element_type=jnp.float32,
        )
        outputs.append(mixed.astype(jnp.bfloat16))
    attended = jnp.concatenate(outputs, axis=2)
    return attended.reshape(row_count, feat_width)


def solution(mesh):
    return jax.shard_map(
        body,
        mesh=mesh,
        in_specs=(P("seq", "head"), P("seq", "head"), P("seq", "head"), P("head", None)),
        out_specs=P("seq", "head"),
        check_vma=False,
    )
```

profile of v0, /device:TPU:33, one launch (start us, length us, event | category | flops | bytes accessed | tf_op | source)
XLA Modules:
  0.0 164.1 jit_solution(3358045583088337417)
XLA Ops:
  0.0 3.8 %collective-permute-start = (bf16[256,256]{1,0:T(8,128)(2,1)}, bf16[256,256]{1,0:T(8,128)(2,1)S(1)}, u32[]{:S(2)}, u32[]{:S(2)}) collective-permute-start(bf16[256,256]{1,0:T(8,128)(2,1)} %param.7), channel_id=1, source_target_pairs={{0,8},{8,16},{16,24},{24,32},{32,40},{40,48},{48,56},{56,64},{64,7... | collective-permute-start | bytes 393224 | tf_op jit(solution)/shard_map/ppermute | solution.py:41
  3.8 1.0 convert_reduce_fusion
  4.8 0.7 broadcast_in_dim.35
  5.4 19.7 %all-to-all-start.2 = ((f32[64,1,256]{2,1,0:T(1,128)}), f32[64,1,256]{2,1,0:T(1,128)S(1)}, u32[]{:S(2)}, u32[]{:S(2)}) async-start(f32[64,1,256]{2,1,0:T(1,128)} %broadcast_in_dim.35), calls=%async_computation.2 | async-start | bytes 131072 | tf_op jit(solution)/shard_map/all_to_all | solution.py:46
  25.1 3.5 %collective-permute-start.1 = (bf16[256,256]{1,0:T(8,128)(2,1)S(1)}, bf16[256,256]{1,0:T(8,128)(2,1)S(1)}, u32[]{:S(2)}, u32[]{:S(2)}) collective-permute-start(bf16[256,256]{1,0:T(8,128)(2,1)S(1)} %copy-done.2), channel_id=1, source_target_pairs={{0,8},{8,16},{16,24},{24,32},{32,40},{40,48},{48,56},{56,64},{64,7... | collective-permute-start | bytes 393224 | tf_op jit(solution)/shard_map/ppermute | solution.py:41
  28.8 0.9 copy-done
  29.7 0.7 copy-done.3
  30.6 0.8 pad_maximum_fusion
  32.1 9.9 %all-to-all-done.2 = f32[64,1,256]{2,1,0:T(1,128)S(1)} async-done(((f32[64,1,256]{2,1,0:T(1,128)}), f32[64,1,256]{2,1,0:T(1,128)S(1)}, u32[]{:S(2)}, u32[]{:S(2)}) %all-to-all-start.2) | async-done | bytes 65568 | tf_op jit(solution)/shard_map/all_to_all | solution.py:46
  42.1 0.6 broadcast_in_dim.36
  42.8 5.5 %all-to-all-start.3 = ((f32[8,1,64]{2,1,0:T(1,128)}), f32[8,1,64]{2,1,0:T(1,128)S(1)}, u32[]{:S(2)}, u32[]{:S(2)}) async-start(f32[8,1,64]{2,1,0:T(1,128)} %broadcast_in_dim.36), calls=%async_computation.3 | async-start | bytes 8192 | tf_op jit(solution)/shard_map/all_to_all | solution.py:46
  48.5 7.7 %all-to-all-done.3 = f32[8,1,64]{2,1,0:T(1,128)S(1)} async-done(((f32[8,1,64]{2,1,0:T(1,128)}), f32[8,1,64]{2,1,0:T(1,128)S(1)}, u32[]{:S(2)}, u32[]{:S(2)}) %all-to-all-start.3) | async-done | bytes 2080 | tf_op jit(solution)/shard_map/all_to_all | solution.py:46
  56.2 0.6 broadcast_in_dim.37
  56.9 7.6 %all-to-all-start.4 = ((f32[64,1,64]{2,1,0:T(1,128)}), f32[64,1,64]{2,1,0:T(1,128)S(1)}, u32[]{:S(2)}, u32[]{:S(2)}) async-start(f32[64,1,64]{2,1,0:T(1,128)} %broadcast_in_dim.37), calls=%async_computation.4 | async-start | bytes 65536 | tf_op jit(solution)/shard_map/all_to_all | solution.py:46
  64.7 16.7 %all-to-all-done.4 = f32[64,1,64]{2,1,0:T(1,128)S(1)} async-done(((f32[64,1,64]{2,1,0:T(1,128)}), f32[64,1,64]{2,1,0:T(1,128)S(1)}, u32[]{:S(2)}, u32[]{:S(2)}) %all-to-all-start.4) | async-done | bytes 16416 | tf_op jit(solution)/shard_map/all_to_all | solution.py:46
  81.4 4.7 %all-to-all-start = ((bf16[1,64,8,256]{3,2,0,1:T(8,128)(2,1)}), bf16[1,64,8,256]{3,2,0,1:T(8,128)(2,1)S(1)}, u32[]{:S(2)}, u32[]{:S(2)}) async-start(bf16[1,64,8,256]{3,2,0,1:T(8,128)(2,1)} %pad_maximum_fusion), calls=%async_computation | async-start | bytes 524288 | tf_op jit(solution)/shard_map/all_to_all | solution.py:20
  90.9 21.7 %all-to-all-done = bf16[1,64,8,256]{3,2,0,1:T(8,128)(2,1)S(1)} async-done(((bf16[1,64,8,256]{3,2,0,1:T(8,128)(2,1)}), bf16[1,64,8,256]{3,2,0,1:T(8,128)(2,1)S(1)}, u32[]{:S(2)}, u32[]{:S(2)}) %all-to-all-start) | async-done | bytes 262176 | tf_op jit(solution)/shard_map/all_to_all | solution.py:20
  112.8 0.7 gather_fusion.1
  113.5 0.7 gather_fusion.3
  114.1 0.7 gather_fusion.2
  114.8 0.7 gather_fusion.4
  115.7 0.7 maximum_bitcast_fusion
  116.4 4.4 %all-to-all-start.1 = ((bf16[64,1,4,256]{3,2,1,0:T(4,128)(2,1)}), bf16[64,1,4,256]{3,2,1,0:T(4,128)(2,1)S(1)}, u32[]{:S(2)}, u32[]{:S(2)}) async-start(bf16[64,1,4,256]{3,2,1,0:T(4,128)(2,1)} %maximum_bitcast_fusion), calls=%async_computation.1 | async-start | bytes 262144 | tf_op jit(solution)/shard_map/all_to_all | solution.py:105
  120.9 0.6 gather_fusion
  121.6 0.6 fusion.39
  122.1 0.7 maximum_bitcast_fusion.1
  122.8 15.7 %all-to-all-done.1 = bf16[64,1,4,256]{3,2,1,0:T(4,128)(2,1)S(1)} async-done(((bf16[64,1,4,256]{3,2,1,0:T(4,128)(2,1)}), bf16[64,1,4,256]{3,2,1,0:T(4,128)(2,1)S(1)}, u32[]{:S(2)}, u32[]{:S(2)}) %all-to-all-start.1) | async-done | bytes 131104 | tf_op jit(solution)/shard_map/all_to_all | solution.py:105
  138.6 4.4 %all-to-all-start.5 = ((bf16[64,1,4,256]{3,2,1,0:T(4,128)(2,1)}), bf16[64,1,4,256]{3,2,1,0:T(4,128)(2,1)S(1)}, u32[]{:S(2)}, u32[]{:S(2)}) async-start(bf16[64,1,4,256]{3,2,1,0:T(4,128)(2,1)} %maximum_bitcast_fusion.1), calls=%async_computation.5 | async-start | bytes 262144 | tf_op jit(solution)/shard_map/all_to_all | solution.py:105
  143.1 0.9 fusion.43
  144.5 16.5 %all-to-all-done.5 = bf16[64,1,4,256]{3,2,1,0:T(4,128)(2,1)S(1)} async-done(((bf16[64,1,4,256]{3,2,1,0:T(4,128)(2,1)}), bf16[64,1,4,256]{3,2,1,0:T(4,128)(2,1)S(1)}, u32[]{:S(2)}, u32[]{:S(2)}) %all-to-all-start.5) | async-done | bytes 131104 | tf_op jit(solution)/shard_map/all_to_all | solution.py:105
  161.3 0.8 fusion.40
  163.4 0.8 copy.26
  (93 shorter events, 8.7 us)
Async XLA Ops:
  0.0 48.2 %collective-permute-start = (bf16[256,256]{1,0:T(8,128)(2,1)}, bf16[256,256]{1,0:T(8,128)(2,1)S(1)}, u32[]{:S(2)}, u32[]{:S(2)}) collective-permute-start(bf16[256,256]{1,0:T(8,128)(2,1)} %param.7), channel_id=1, source_target_pairs={{0,8},{8,16},{16,24},{24,32},{32,40},{40,48},{48,56},{56,64},{64,7... | collective-permute-start | bytes 393224 | tf_op jit(solution)/shard_map/ppermute | solution.py:41
  3.8 21.3 %copy-start.2 = (bf16[256,256]{1,0:T(8,128)(2,1)S(1)}, bf16[256,256]{1,0:T(8,128)(2,1)}, u32[]{:S(2)}) copy-start(bf16[256,256]{1,0:T(8,128)(2,1)} %param.8) | copy-start | bytes 393220
  4.8 23.9 %copy-start.1 = (bf16[256,256]{1,0:T(8,128)(2,1)S(1)}, bf16[256,256]{1,0:T(8,128)(2,1)}, u32[]{:S(2)}) copy-start(bf16[256,256]{1,0:T(8,128)(2,1)} %param.7) | copy-start | bytes 393220
  5.4 36.6 %all-to-all-start.2 = ((f32[64,1,256]{2,1,0:T(1,128)}), f32[64,1,256]{2,1,0:T(1,128)S(1)}, u32[]{:S(2)}, u32[]{:S(2)}) async-start(f32[64,1,256]{2,1,0:T(1,128)} %broadcast_in_dim.35), calls=%async_computation.2 | async-start | bytes 131072 | tf_op jit(solution)/shard_map/all_to_all | solution.py:46
  25.1 137.8 %collective-permute-start.1 = (bf16[256,256]{1,0:T(8,128)(2,1)S(1)}, bf16[256,256]{1,0:T(8,128)(2,1)S(1)}, u32[]{:S(2)}, u32[]{:S(2)}) collective-permute-start(bf16[256,256]{1,0:T(8,128)(2,1)S(1)} %copy-done.2), channel_id=1, source_target_pairs={{0,8},{8,16},{16,24},{24,32},{32,40},{40,48},{48,56},{56,64},{64,7... | collective-permute-start | bytes 393224 | tf_op jit(solution)/shard_map/ppermute | solution.py:41
  28.7 0.9 copy-start
  29.7 0.7 copy-start.3
  42.8 13.4 %all-to-all-start.3 = ((f32[8,1,64]{2,1,0:T(1,128)}), f32[8,1,64]{2,1,0:T(1,128)S(1)}, u32[]{:S(2)}, u32[]{:S(2)}) async-start(f32[8,1,64]{2,1,0:T(1,128)} %broadcast_in_dim.36), calls=%async_computation.3 | async-start | bytes 8192 | tf_op jit(solution)/shard_map/all_to_all | solution.py:46
  56.9 24.6 %all-to-all-start.4 = ((f32[64,1,64]{2,1,0:T(1,128)}), f32[64,1,64]{2,1,0:T(1,128)S(1)}, u32[]{:S(2)}, u32[]{:S(2)}) async-start(f32[64,1,64]{2,1,0:T(1,128)} %broadcast_in_dim.37), calls=%async_computation.4 | async-start | bytes 65536 | tf_op jit(solution)/shard_map/all_to_all | solution.py:46
  81.4 31.2 %all-to-all-start = ((bf16[1,64,8,256]{3,2,0,1:T(8,128)(2,1)}), bf16[1,64,8,256]{3,2,0,1:T(8,128)(2,1)S(1)}, u32[]{:S(2)}, u32[]{:S(2)}) async-start(bf16[1,64,8,256]{3,2,0,1:T(8,128)(2,1)} %pad_maximum_fusion), calls=%async_computation | async-start | bytes 524288 | tf_op jit(solution)/shard_map/all_to_all | solution.py:20
  116.4 22.1 %all-to-all-start.1 = ((bf16[64,1,4,256]{3,2,1,0:T(4,128)(2,1)}), bf16[64,1,4,256]{3,2,1,0:T(4,128)(2,1)S(1)}, u32[]{:S(2)}, u32[]{:S(2)}) async-start(bf16[64,1,4,256]{3,2,1,0:T(4,128)(2,1)} %maximum_bitcast_fusion), calls=%async_computation.1 | async-start | bytes 262144 | tf_op jit(solution)/shard_map/all_to_all | solution.py:105
  138.6 22.4 %all-to-all-start.5 = ((bf16[64,1,4,256]{3,2,1,0:T(4,128)(2,1)}), bf16[64,1,4,256]{3,2,1,0:T(4,128)(2,1)S(1)}, u32[]{:S(2)}, u32[]{:S(2)}) async-start(bf16[64,1,4,256]{3,2,1,0:T(4,128)(2,1)} %maximum_bitcast_fusion.1), calls=%async_computation.5 | async-start | bytes 262144 | tf_op jit(solution)/shard_map/all_to_all | solution.py:105
where the time goes:
time: 165 us; the launch traced here: 164 us
  waiting for transfers between devices  88.3 us (54%)
  starting transfers between devices  53.7 us (33%)
  other arithmetic  9.13 us (6%)
  local copies, waits for them, and re-layouts  8.41 us (5%)
  matrix products  4.27 us (3%)
    all_to_all x3, waiting for transfers between devices, from_everyone(): return lax.all_to_all(copies, axis, split_axis=0, concat_axis=0, tiled=True)  34.4 us
    all_to_all x3, starting transfers between devices, from_everyone(): return lax.all_to_all(copies, axis, split_axis=0, concat_axis=0, tiled=True)  32.8 us
    all_to_all x2, waiting for transfers between devices, fetch_partners(): lax.all_to_all(shortened(picked), 'seq', split_axis=0, concat_axis=2, til...  32.2 us
    all_to_all x1, waiting for transfers between devices, side_by_side(): lax.all_to_all(both, axis, split_axis=split_dim, concat_axis=concat_dim,...  21.7 us
    all_to_all x2, starting transfers between devices, fetch_partners(): lax.all_to_all(shortened(picked), 'seq', split_axis=0, concat_axis=2, til...  8.89 us
    ppermute x2, starting transfers between devices, shifted(): return lax.ppermute(block, axis, route)  7.3 us
    all_to_all x1, starting transfers between devices, side_by_side(): lax.all_to_all(both, axis, split_axis=split_dim, concat_axis=concat_dim,...  4.71 us
  transfers between devices with their start and end apart: 8, of which 6 were waited for; matrix products, arithmetic and copies ran while one was open for 12% of the time, Pallas kernels for 0%

commit v1 on v0

v1 whole, which is shorter than its diff:
```python
import functools
import math

import jax
import jax.numpy as jnp
from jax import lax
from jax.experimental import pallas as pl
from jax.experimental.pallas import tpu as pltpu
from jax.sharding import PartitionSpec as P

DH = 128
BS = 256
SINK_ITERS = 8
SHARPNESS = 2.0
CHUNKS = 4
HIGHEST = lax.Precision.HIGHEST
MESH = pl.DeviceIdType.MESH


def bytes_wait(ref, sem):
    pltpu.make_async_copy(ref, ref, sem).wait()


def exchange_kernel(
    plane,
    groups,
    partner,
    q_hbm,
    k_hbm,
    v_hbm,
    part_out,
    prev_out,
    plan_out,
    qs,
    kv,
    held_a,
    held_b,
    pick,
    pk_all,
    pq,
    parts,
    rows_all,
    load_sem,
    own_sem,
    pk_send,
    pk_recv,
    fwd_send,
    fwd_recv,
    mir_send,
    mir_recv,
    head_send,
    head_recv,
    row_send,
    row_recv,
    spread_send,
    spread_recv,
    z_send,
    z_recv,
    back_send,
    back_recv,
    prev_send,
    extra_send,
    prev_recv,
):
    held = (held_a, held_b)
    s = lax.axis_index("seq")
    g = lax.axis_index("head")
    p = s // plane
    i = s % plane
    base = p * plane
    mirror = (s + plane) % (2 * plane)
    half = plane // 2
    step = plane // CHUNKS
    before = (base + 2 * plane - 1) % (2 * plane)

    def peer(o):
        j = (i + o) % plane
        return j, base + j

    def remote(src, dst, ss, rs, seq, head=None):
        return pltpu.make_async_remote_copy(
            src_ref=src,
            dst_ref=dst,
            send_sem=ss,
            recv_sem=rs,
            device_id=(seq, g if head is None else head),
            device_id_type=MESH,
        )

    def each_peer(body):
        def wrapped(o, c):
            body(*peer(o))
            return c

        lax.fori_loop(1, plane, wrapped, 0)

    def each_group(body):
        def wrapped(o, c):
            body((g + o) % groups)
            return c

        lax.fori_loop(1, groups, wrapped, 0)

    barrier = pltpu.get_barrier_semaphore()
    pl.semaphore_signal(barrier, inc=1, device_id=(mirror, g), device_id_type=MESH)
    each_group(
        lambda og: pl.semaphore_signal(barrier, inc=1, device_id=(s, og), device_id_type=MESH)
    )
    each_peer(
        lambda j, d: pl.semaphore_signal(barrier, inc=1, device_id=(d, g), device_id_type=MESH)
    )

    loads = (
        pltpu.make_async_copy(q_hbm, qs, load_sem.at[0]),
        pltpu.make_async_copy(k_hbm, kv.at[pl.ds(0, half)], load_sem.at[1]),
        pltpu.make_async_copy(v_hbm, kv.at[pl.ds(half, half)], load_sem.at[2]),
    )
    for c in loads:
        c.start()
    for c in loads:
        c.wait()
    pooled_q = jnp.sum(jnp.sum(qs[...].astype(jnp.float32), axis=0), axis=0, keepdims=True)
    pooled_k = jnp.sum(
        jnp.sum(kv[pl.ds(0, half)].astype(jnp.float32), axis=0), axis=0, keepdims=True
    )
    for h in range(2):
        lanes = slice(h * DH, (h + 1) * DH)
        pq[0, h : h + 1, :] = pooled_q[:, lanes] / math.sqrt(BS)
        pk_all[s, h : h + 1, :] = pooled_k[:, lanes] / math.sqrt(BS)

    pl.semaphore_wait(barrier, plane - 1 + 1 + groups - 1)

    to_mirror = (
        remote(pk_all.at[s], pk_all.at[s], mir_send.at[0], mir_recv.at[0], mirror),
        remote(pq.at[0], pq.at[1], mir_send.at[1], mir_recv.at[1], mirror),
    )
    for c in to_mirror:
        c.start()

    def spread(h):
        lanes = pl.ds(h * DH, DH)
        pltpu.make_async_copy(kv.at[i, :, lanes], held[h].at[s], spread_recv.at[h]).start()
        each_peer(
            lambda j, d: remote(
                kv.at[j, :, lanes], held[h].at[s], spread_send.at[h], spread_recv.at[h], d
            ).start()
        )

    def exchange(h, c):
        rows = pl.ds(base + c * step, step)
        return remote(
            held[h].at[rows], held[h].at[rows], z_send.at[h, c], z_recv.at[h, c], mirror
        )

    def arrived(h, c):
        rows = pl.ds((plane - base) + c * step, step)
        bytes_wait(held[h].at[rows], z_recv.at[h, c])

    spread(0)
    each_peer(lambda j, d: remote(pk_all.at[s], pk_all.at[s], pk_send, pk_recv, d).start())
    spread(1)

    @pl.when(i < plane - 1)
    def _():
        for h in range(2):
            lanes = pl.ds(h * DH, DH)
            remote(
                kv.at[:, :, lanes], prev_out.at[h], prev_send.at[h], prev_recv.at[h], s + 1
            ).start()

    bytes_wait(held[0].at[pl.ds(0, plane)], spread_recv.at[0])
    exchange(0, 0).start()
    exchange(0, 1).start()
    for c in to_mirror:
        c.wait_recv()
    each_peer(
        lambda j, d: remote(
            pk_all.at[mirror], pk_all.at[mirror], fwd_send, fwd_recv, d
        ).start()
    )
    bytes_wait(held[1].at[pl.ds(0, plane)], spread_recv.at[1])
    exchange(0, 2).start()

    bytes_wait(pk_all.at[pl.ds(0, plane - 1)], pk_recv)
    bytes_wait(pk_all.at[pl.ds(0, plane - 1)], fwd_recv)
    total = jnp.zeros((2, 2 * plane), jnp.float32)
    for h in range(2):
        total = total + lax.dot_general(
            pq[:, h, :],
            pk_all[:, h, :],
            (((1,), (1,)), ((), ())),
            precision=HIGHEST,
            preferred_element_type=jnp.float32,
        )
    total = total * (SHARPNESS / math.sqrt(2 * DH * groups))
    parts[g, :, 0 : 2 * plane] = total
    each_group(
        lambda og: remote(parts.at[g], parts.at[g], head_send, head_recv, s, og).start()
    )
    exchange(0, 3).start()
    for c in range(CHUNKS):
        exchange(1, c).start()

    bytes_wait(parts.at[pl.ds(0, groups - 1)], head_recv)
    rows_all[i] = jnp.sum(parts[...], axis=0)
    each_peer(lambda j, d: remote(rows_all.at[i], rows_all.at[i], row_send, row_recv, d).start())

    def give_back(h):
        for c in range(CHUNKS):
            arrived(h, c)

        def choose(j, carry):
            pick[h, j] = held[h][partner[h, base + j]]
            return carry

        lax.fori_loop(0, plane, choose, 0)
        each_peer(
            lambda j, d: remote(
                pick.at[h, j], part_out.at[h, i], back_send.at[h], back_recv.at[h], d
            ).start()
        )
        pltpu.make_async_copy(pick.at[h, i], part_out.at[h, i], back_recv.at[h]).start()

        @pl.when(i == 0)
        def _():
            pltpu.make_async_copy(held[h].at[before], prev_out.at[h, 0], prev_recv.at[h]).start()

        @pl.when(i > 0)
        def _():
            remote(
                held[h].at[before],
                prev_out.at[h, i],
                extra_send.at[h],
                prev_recv.at[h],
                base,
            ).start()

    give_back(0)

    bytes_wait(rows_all.at[pl.ds(0, plane - 1)], row_recv)
    plan = jnp.concatenate([rows_all[:, 0, :], rows_all[:, 1, :]], axis=0)[:, : 2 * plane]

    def sweep(_, x):
        for along in (1, 0):
            top = jnp.max(x, axis=along, keepdims=True)
            x = x - (top + jnp.log(jnp.sum(jnp.exp(x - top), axis=along, keepdims=True)))
        return x

    plan_out[...] = lax.fori_loop(0, SINK_ITERS, sweep, plan)

    give_back(1)

    for h in range(2):
        bytes_wait(part_out.at[h], back_recv.at[h])
        bytes_wait(prev_out.at[h], prev_recv.at[h])
        bytes_wait(held[h].at[pl.ds(0, plane - 1)], spread_send.at[h])
        bytes_wait(pick.at[h, pl.ds(0, plane - 1)], back_send.at[h])
        for c in range(CHUNKS):
            exchange(h, c).wait_send()
    for c in to_mirror:
        c.wait_send()
    bytes_wait(pk_all.at[pl.ds(0, plane - 1)], pk_send)
    bytes_wait(pk_all.at[pl.ds(0, plane - 1)], fwd_send)
    bytes_wait(parts.at[pl.ds(0, groups - 1)], head_send)
    bytes_wait(rows_all.at[pl.ds(0, plane - 1)], row_send)

    @pl.when(i < plane - 1)
    def _():
        for h in range(2):
            bytes_wait(prev_out.at[h], prev_send.at[h])

    @pl.when(i > 0)
    def _():
        for h in range(2):
            bytes_wait(held[h].at[0], extra_send.at[h])


def attend_kernel(plane, partner, q_ref, k_ref, v_ref, part, prev, plan, out_ref):
    s = lax.axis_index("seq")
    i = s % plane
    half = plane // 2
    inv_scale = 1.0 / math.sqrt(DH)
    log_plan = plan[...]
    row_id = lax.broadcasted_iota(jnp.int32, log_plan.shape, 0)
    col_id = lax.broadcasted_iota(jnp.int32, log_plan.shape, 1)
    for h in range(2):
        lanes = slice(h * DH, (h + 1) * DH)
        chosen = (row_id == i) & (col_id == partner[h, s])
        bias = math.log(2 * plane) + jnp.sum(jnp.where(chosen, log_plan, 0.0))
        q = q_ref[:, lanes]
        keys = (
            prev[h, 0:half].reshape(BS, DH),
            k_ref[:, lanes],
            part[h, 0:half].reshape(BS, DH),
        )
        vals = (
            prev[h, half:plane].reshape(BS, DH),
            v_ref[:, lanes],
            part[h, half:plane].reshape(BS, DH),
        )
        logits = [
            lax.dot_general(q, key, (((1,), (1,)), ((), ())), preferred_element_type=jnp.float32)
            * inv_scale
            for key in keys
        ]
        logits[0] = jnp.where(s > 0, logits[0], -jnp.inf)
        logits[2] = logits[2] + bias
        top = jnp.maximum(jnp.maximum(logits[0], logits[1]), logits[2])
        top = jnp.max(top, axis=1, keepdims=True)
        expo = [jnp.exp(x - top) for x in logits]
        denom = jnp.sum(expo[0] + expo[1] + expo[2], axis=1, keepdims=True)
        inverse = 1.0 / denom
        mixed = jnp.zeros((BS, DH), jnp.float32)
        for e, val in zip(expo, vals):
            mixed = mixed + jnp.dot(
                (e * inverse).astype(jnp.bfloat16), val, preferred_element_type=jnp.float32
            )
        out_ref[:, lanes] = mixed.astype(jnp.bfloat16)


def solution(mesh):
    seq, groups = mesh.shape["seq"], mesh.shape["head"]
    plane = seq // 2
    piece = 2 * BS // plane
    half = plane // 2
    width = 2 * DH

    def body(queries, keys, values, partner):
        vmem = pl.BlockSpec(memory_space=pltpu.VMEM)
        smem = pl.BlockSpec(memory_space=pltpu.SMEM)
        hbm = pl.BlockSpec(memory_space=pl.ANY)
        dma = pltpu.SemaphoreType.DMA
        blocks = jax.ShapeDtypeStruct((2, plane, piece, DH), jnp.bfloat16)
        folded = (half, piece, width)
        part, prev, plan = pl.pallas_call(
            functools.partial(exchange_kernel, plane, groups),
            out_shape=(blocks, blocks, jax.ShapeDtypeStruct((seq, seq), jnp.float32)),
            in_specs=[smem, hbm, hbm, hbm],
            out_specs=(vmem, vmem, vmem),
            scratch_shapes=[
                pltpu.VMEM(folded, jnp.bfloat16),
                pltpu.VMEM((plane, piece, width), jnp.bfloat16),
                pltpu.VMEM((seq, piece, DH), jnp.bfloat16),
                pltpu.VMEM((seq, piece, DH), jnp.bfloat16),
                pltpu.VMEM((2, plane, piece, DH), jnp.bfloat16),
                pltpu.VMEM((seq, 2, DH), jnp.float32),
                pltpu.VMEM((2, 2, DH), jnp.float32),
                pltpu.VMEM((groups, 2, DH), jnp.float32),
                pltpu.VMEM((plane, 2, DH), jnp.float32),
                dma((3,)),
                dma(()),
                dma(()),
                dma(()),
                dma(()),
                dma(()),
                dma((2,)),
                dma((2,)),
                dma(()),
                dma(()),
                dma(()),
                dma(()),
                dma((2,)),
                dma((2,)),
                dma((2, CHUNKS)),
                dma((2, CHUNKS)),
                dma((2,)),
                dma((2,)),
                dma((2,)),
                dma((2,)),
                dma((2,)),
            ],
            compiler_params=pltpu.CompilerParams(collective_id=0, has_side_effects=True),
            name="exchange",
        )(partner, queries.reshape(folded), keys.reshape(folded), values.reshape(folded))
        return pl.pallas_call(
            functools.partial(attend_kernel, plane),
            out_shape=jax.ShapeDtypeStruct(queries.shape, queries.dtype),
            in_specs=[smem] + [vmem] * 6,
            out_specs=vmem,
            name="attend",
        )(partner, queries, keys, values, part, prev, plan)

    return jax.shard_map(
        body,
        mesh=mesh,
        in_specs=(P("seq", "head"), P("seq", "head"), P("seq", "head"), P("head", None)),
        out_specs=P("seq", "head"),
        check_vma=False,
    )
```

time: 165 us -> 62.7 us (0.38)
  the two profiles are of different devices: /device:TPU:33 before, /device:TPU:96 now
where the time goes in v1:
time: 62.7 us; the launch traced here: 62.5 us
  Pallas kernels  62.5 us (100%)
    pallas_call x1, Pallas kernels, body(): pl.pallas_call(functools.partial(exchange_kernel, plane, groups), out_sha...  59.4 us
    pallas_call x1, Pallas kernels, body(): pl.pallas_call(functools.partial(attend_kernel, plane), out_shape=jax.Sha...  3.14 us

profile of v1, /device:TPU:96, one launch (start us, length us, event | category | flops | bytes accessed | tf_op | source)
XLA Modules:
  0.0 62.5 jit_solution(261487841527477171)
XLA Ops:
  0.0 59.4 %exchange.1 = (bf16[2,32,16,128]{3,2,1,0:T(8,128)(2,1)}, bf16[2,32,16,128]{3,2,1,0:T(8,128)(2,1)}, f32[64,64]{1,0:T(8,128)}) custom-call(s32[2,64]{1,0:T(2,128)} %partner.3, bf16[16,16,256]{2,1,0:T(8,128)(2,1)} %bitcast.3, bf16[16,16,256]{2,1,0:T(8,128)(2,1)} %bitcast.4, bf16[16,16,256]{2,1,0:T(8,128)(2,1)} %bitcast.5), custom_call_target="tpu_custom_call" | custom-call | tf_op jit(solution)/shard_map/exchange/pallas_call | solution.py:335
  59.4 3.1 %attend.1 = bf16[256,256]{1,0:T(8,128)(2,1)} custom-call(s32[2,64]{1,0:T(2,128)} %partner.3, bf16[256,256]{1,0:T(8,128)(2,1)} %q_ref.1, bf16[256,256]{1,0:T(8,128)(2,1)} %k_ref.1, bf16[256,256]{1,0:T(8,128)(2,1)} %v_ref.1, bf16[2,32,16,128]{3,2,1,0:T(8,128)(2,1)} %get-tuple-element.8.part, bf16[2,32,16,128]{3,2,1,0:T(8,128)(2,1)} %get-tuple-element.9.prev, ...), custom_call_target="tpu_custom_call" | custom-call | tf_op jit(solution)/shard_map/attend/pallas_call | solution.py:375

commit v2 on v1

v2 whole, which is shorter than its diff:
```python
import functools
import math

import jax
import jax.numpy as jnp
from jax import lax
from jax.experimental import pallas as pl
from jax.experimental.pallas import tpu as pltpu
from jax.sharding import PartitionSpec as P

DH = 128
BS = 256
SINK_ITERS = 8
SHARPNESS = 2.0
CHUNKS = 4
HIGHEST = lax.Precision.HIGHEST
MESH = pl.DeviceIdType.MESH


def bytes_wait(ref, sem):
    pltpu.make_async_copy(ref, ref, sem).wait()


def sparse_attention_kernel(
    plane,
    groups,
    partner,
    q_hbm,
    k_hbm,
    v_hbm,
    out,
    qs,
    kv,
    held_a,
    held_b,
    pick,
    part,
    prev,
    pk_all,
    pq,
    parts,
    rows_all,
    bias,
    top_all,
    den_all,
    mix_all,
    load_sem,
    pk_send,
    pk_recv,
    fwd_send,
    fwd_recv,
    mir_send,
    mir_recv,
    head_send,
    head_recv,
    row_send,
    row_recv,
    bias_send,
    bias_recv,
    spread_send,
    spread_recv,
    z_send,
    z_recv,
    back_send,
    back_recv,
    prev_send,
    extra_send,
    prev_recv,
    ready,
):
    held = (held_a, held_b)
    s = lax.axis_index("seq")
    g = lax.axis_index("head")
    p = s // plane
    i = s % plane
    base = p * plane
    mirror = (s + plane) % (2 * plane)
    half = plane // 2
    step = plane // CHUNKS
    before = (base + 2 * plane - 1) % (2 * plane)
    inv_scale = 1.0 / math.sqrt(DH)

    def remote(src, dst, ss, rs, seq, head=None):
        return pltpu.make_async_remote_copy(
            src_ref=src,
            dst_ref=dst,
            send_sem=ss,
            recv_sem=rs,
            device_id=(seq, g if head is None else head),
            device_id_type=MESH,
        )

    def signal(sem, seq, head=None):
        pl.semaphore_signal(
            sem,
            inc=1,
            device_id=(seq, g if head is None else head),
            device_id_type=MESH,
        )

    def each_peer(body):
        def wrapped(o, c):
            j = (i + o) % plane
            body(j, base + j)
            return c

        lax.fori_loop(1, plane, wrapped, 0)

    def each_group(body):
        def wrapped(o, c):
            body((g + o) % groups)
            return c

        lax.fori_loop(1, groups, wrapped, 0)

    barrier = pltpu.get_barrier_semaphore()

    @pl.when(p == 0)
    def _():
        signal(barrier, mirror)
        each_group(lambda og: signal(barrier, s, og))

    each_peer(lambda j, d: signal(barrier, d))

    loads = (
        pltpu.make_async_copy(q_hbm, qs, load_sem.at[0]),
        pltpu.make_async_copy(k_hbm, kv.at[pl.ds(0, half)], load_sem.at[1]),
        pltpu.make_async_copy(v_hbm, kv.at[pl.ds(half, half)], load_sem.at[2]),
    )
    for c in loads:
        c.start()
    for c in loads:
        c.wait()
    pooled_q = jnp.sum(jnp.sum(qs[...].astype(jnp.float32), axis=0), axis=0, keepdims=True)
    pooled_k = jnp.sum(
        jnp.sum(kv[pl.ds(0, half)].astype(jnp.float32), axis=0), axis=0, keepdims=True
    )
    for h in range(2):
        lanes = slice(h * DH, (h + 1) * DH)
        pq[0, h : h + 1, :] = pooled_q[:, lanes] / math.sqrt(BS)
        pk_all[s, h : h + 1, :] = pooled_k[:, lanes] / math.sqrt(BS)

    to_mirror = (
        remote(pk_all.at[s], pk_all.at[s], mir_send.at[0], mir_recv.at[0], mirror),
        remote(pq.at[0], pq.at[1], mir_send.at[1], mir_recv.at[1], mirror),
    )
    bias_copy = remote(bias.at[1], bias.at[0], bias_send, bias_recv, mirror)

    def spread(h):
        lanes = pl.ds(h * DH, DH)
        pltpu.make_async_copy(kv.at[i, :, lanes], held[h].at[s], spread_recv.at[h]).start()
        each_peer(
            lambda j, d: remote(
                kv.at[j, :, lanes], held[h].at[s], spread_send.at[h], spread_recv.at[h], d
            ).start()
        )

    def hand_on():
        @pl.when(i < plane - 1)
        def _():
            for h in range(2):
                lanes = pl.ds(h * DH, DH)
                remote(
                    kv.at[:, :, lanes], prev.at[h], prev_send.at[h], prev_recv.at[h], s + 1
                ).start()

    def exchange(h, c):
        rows = pl.ds(base + c * step, step)
        return remote(
            held[h].at[rows], held[h].at[rows], z_send.at[h, c], z_recv.at[h, c], mirror
        )

    def spread_done(h):
        bytes_wait(held[h].at[pl.ds(0, plane)], spread_recv.at[h])

    def give_back(h):
        for c in range(CHUNKS):
            rows = pl.ds((plane - base) + c * step, step)
            bytes_wait(held[h].at[rows], z_recv.at[h, c])

        def choose(j, carry):
            pick[h, j] = held[h][partner[h, base + j]]
            return carry

        lax.fori_loop(0, plane, choose, 0)
        each_peer(
            lambda j, d: remote(
                pick.at[h, j], part.at[h, i], back_send.at[h], back_recv.at[h], d
            ).start()
        )
        pltpu.make_async_copy(pick.at[h, i], part.at[h, i], back_recv.at[h]).start()

        @pl.when(i == 0)
        def _():
            pltpu.make_async_copy(held[h].at[before], prev.at[h, 0], prev_recv.at[h]).start()

        @pl.when(i > 0)
        def _():
            remote(
                held[h].at[before], prev.at[h, i], extra_send.at[h], prev_recv.at[h], base
            ).start()

    def query(h):
        return qs[:, :, h * DH : (h + 1) * DH].reshape(BS, DH)

    def scored(h, key):
        x = lax.dot_general(
            query(h), key, (((1,), (1,)), ((), ())), preferred_element_type=jnp.float32
        )
        return x * inv_scale

    def stacked(ref, h):
        return (
            ref[h, 0:half].reshape(BS, DH),
            ref[h, half:plane].reshape(BS, DH),
        )

    def local():
        for h in range(2):
            lanes = slice(h * DH, (h + 1) * DH)
            x = scored(h, kv[0:half, :, lanes].reshape(BS, DH))
            top = jnp.max(x, axis=1, keepdims=True)
            e = jnp.exp(x - top)
            top_all[h] = top
            den_all[h] = jnp.sum(e, axis=1, keepdims=True)
            mix_all[h] = jnp.dot(
                e.astype(jnp.bfloat16),
                kv[half:plane, :, lanes].reshape(BS, DH),
                preferred_element_type=jnp.float32,
            )

    def merged(h, ref, shift):
        key, val = stacked(ref, h)
        x = scored(h, key)
        if shift is not None:
            x = x + shift
        old = top_all[h]
        top = jnp.maximum(old, jnp.max(x, axis=1, keepdims=True))
        keep = jnp.exp(old - top)
        e = jnp.exp(x - top)
        den = den_all[h] * keep + jnp.sum(e, axis=1, keepdims=True)
        mix = mix_all[h] * keep + jnp.dot(
            e.astype(jnp.bfloat16), val, preferred_element_type=jnp.float32
        )
        return top, den, mix

    def previous(h):
        top, den, mix = merged(h, prev, None)
        top_all[h] = top
        den_all[h] = den
        mix_all[h] = mix

    def early_previous():
        @pl.when(i > 0)
        def _():
            for h in range(2):
                bytes_wait(prev.at[h], prev_recv.at[h])
                previous(h)

    def late_previous(h):
        @pl.when(i == 0)
        def _():
            bytes_wait(prev.at[h], prev_recv.at[h])

        @pl.when(s == plane)
        def _():
            previous(h)

    def finish(h):
        late_previous(h)
        bytes_wait(part.at[h], back_recv.at[h])
        _, den, mix = merged(h, part, bias[0, h : h + 1, 0:1])
        out[:, h * DH : (h + 1) * DH] = (mix * (1.0 / den)).astype(jnp.bfloat16)

    def scores():
        total = jnp.zeros((2, 2 * plane), jnp.float32)
        for h in range(2):
            total = total + lax.dot_general(
                pq[:, h, :],
                pk_all[:, h, :],
                (((1,), (1,)), ((), ())),
                precision=HIGHEST,
                preferred_element_type=jnp.float32,
            )
        parts[g, :, 0 : 2 * plane] = total * (SHARPNESS / math.sqrt(2 * DH * groups))

    def sinkhorn():
        x = jnp.concatenate([rows_all[:, 0, :], rows_all[:, 1, :]], axis=0)[:, : 2 * plane]

        def sweep(_, x):
            for along in (1, 0):
                top = jnp.max(x, axis=along, keepdims=True)
                x = x - (top + jnp.log(jnp.sum(jnp.exp(x - top), axis=along, keepdims=True)))
            return x

        x = lax.fori_loop(0, SINK_ITERS, sweep, x)
        row = lax.broadcasted_iota(jnp.int32, x.shape, 0)
        col = lax.broadcasted_iota(jnp.int32, x.shape, 1)
        for which, block in ((0, s), (1, mirror)):
            for h in range(2):
                chosen = (row == i + which * plane) & (col == partner[h, block])
                value = jnp.sum(
                    jnp.sum(jnp.where(chosen, x, 0.0), axis=1, keepdims=True), axis=0, keepdims=True
                )
                bias[which, h : h + 1, :] = jnp.broadcast_to(
                    value + math.log(2 * plane), (1, DH)
                )

    @pl.when(p == 0)
    def _():
        pl.semaphore_wait(barrier, plane - 1 + groups - 1)
        spread(0)
        each_peer(lambda j, d: remote(pk_all.at[s], pk_all.at[s], pk_send, pk_recv, d).start())
        spread(1)
        hand_on()
        local()
        spread_done(0)
        pl.semaphore_wait(ready, 1)
        exchange(0, 0).start()
        exchange(0, 1).start()
        for c in to_mirror:
            c.wait_recv()
        each_peer(
            lambda j, d: remote(
                pk_all.at[mirror], pk_all.at[mirror], fwd_send, fwd_recv, d
            ).start()
        )
        spread_done(1)
        bytes_wait(pk_all.at[pl.ds(0, plane - 1)], pk_recv)
        bytes_wait(pk_all.at[pl.ds(0, plane - 1)], fwd_recv)
        scores()
        each_group(
            lambda og: remote(parts.at[g], parts.at[g], head_send, head_recv, s, og).start()
        )
        for c in range(2, CHUNKS):
            exchange(0, c).start()
        for c in range(CHUNKS):
            exchange(1, c).start()
        early_previous()
        bytes_wait(parts.at[pl.ds(0, groups - 1)], head_recv)
        rows_all[i] = jnp.sum(parts[...], axis=0)
        each_peer(
            lambda j, d: remote(rows_all.at[i], rows_all.at[i], row_send, row_recv, d).start()
        )
        give_back(0)
        bytes_wait(rows_all.at[pl.ds(0, plane - 1)], row_recv)
        sinkhorn()
        bias_copy.start()
        finish(0)
        give_back(1)
        finish(1)
        bytes_wait(pk_all.at[pl.ds(0, plane - 1)], pk_send)
        bytes_wait(pk_all.at[pl.ds(0, plane - 1)], fwd_send)
        bytes_wait(parts.at[pl.ds(0, groups - 1)], head_send)
        bytes_wait(rows_all.at[pl.ds(0, plane - 1)], row_send)
        bias_copy.wait_send()

    @pl.when(p == 1)
    def _():
        pl.semaphore_wait(barrier, plane - 1 + 1)
        signal(ready, mirror)
        for c in to_mirror:
            c.start()
        spread(0)
        spread(1)
        hand_on()
        for h in range(2):
            spread_done(h)
            for c in range(CHUNKS):
                exchange(h, c).start()
        local()
        early_previous()
        give_back(0)
        give_back(1)
        bias_copy.wait_recv()
        finish(0)
        finish(1)
        for c in to_mirror:
            c.wait_send()

    for h in range(2):
        bytes_wait(held[h].at[pl.ds(0, plane - 1)], spread_send.at[h])
        bytes_wait(pick.at[h, pl.ds(0, plane - 1)], back_send.at[h])
        for c in range(CHUNKS):
            exchange(h, c).wait_send()

    @pl.when(i < plane - 1)
    def _():
        for h in range(2):
            bytes_wait(prev.at[h], prev_send.at[h])

    @pl.when(i > 0)
    def _():
        for h in range(2):
            bytes_wait(held[h].at[0], extra_send.at[h])


def solution(mesh):
    seq, groups = mesh.shape["seq"], mesh.shape["head"]
    plane = seq // 2
    piece = 2 * BS // plane
    half = plane // 2
    width = 2 * DH

    def body(queries, keys, values, partner):
        hbm = pl.BlockSpec(memory_space=pl.ANY)
        dma = pltpu.SemaphoreType.DMA
        folded = (half, piece, width)
        pieces = pltpu.VMEM((2, plane, piece, DH), jnp.bfloat16)
        return pl.pallas_call(
            functools.partial(sparse_attention_kernel, plane, groups),
            out_shape=jax.ShapeDtypeStruct(queries.shape, queries.dtype),
            in_specs=[pl.BlockSpec(memory_space=pltpu.SMEM), hbm, hbm, hbm],
            out_specs=pl.BlockSpec(memory_space=pltpu.VMEM),
            scratch_shapes=[
                pltpu.VMEM(folded, jnp.bfloat16),
                pltpu.VMEM((plane, piece, width), jnp.bfloat16),
                pltpu.VMEM((seq, piece, DH), jnp.bfloat16),
                pltpu.VMEM((seq, piece, DH), jnp.bfloat16),
                pieces,
                pieces,
                pieces,
                pltpu.VMEM((seq, 2, DH), jnp.float32),
                pltpu.VMEM((2, 2, DH), jnp.float32),
                pltpu.VMEM((groups, 2, DH), jnp.float32),
                pltpu.VMEM((plane, 2, DH), jnp.float32),
                pltpu.VMEM((2, 2, DH), jnp.float32),
                pltpu.VMEM((2, BS, 1), jnp.float32),
                pltpu.VMEM((2, BS, 1), jnp.float32),
                pltpu.VMEM((2, BS, DH), jnp.float32),
                dma((3,)),
                dma(()),
                dma(()),
                dma(()),
                dma(()),
                dma((2,)),
                dma((2,)),
                dma(()),
                dma(()),
                dma(()),
                dma(()),
                dma(()),
                dma(()),
                dma((2,)),
                dma((2,)),
                dma((2, CHUNKS)),
                dma((2, CHUNKS)),
                dma((2,)),
                dma((2,)),
                dma((2,)),
                dma((2,)),
                dma((2,)),
                pltpu.SemaphoreType.REGULAR,
            ],
            compiler_params=pltpu.CompilerParams(collective_id=0, has_side_effects=True),
            name="sparse_attention",
        )(partner, queries.reshape(folded), keys.reshape(folded), values.reshape(folded))

    return jax.shard_map(
        body,
        mesh=mesh,
        in_specs=(P("seq", "head"), P("seq", "head"), P("seq", "head"), P("head", None)),
        out_specs=P("seq", "head"),
        check_vma=False,
    )
```

time: 62.7 us -> 60.4 us (0.963)
  the two profiles are of different devices: /device:TPU:96 before, /device:TPU:160 now
where the time goes in v2:
time: 60.4 us; the launch traced here: 60.3 us
  Pallas kernels  58.7 us (97%)
  local copies, waits for them, and re-layouts  1.57 us (3%)
    pallas_call x1, Pallas kernels, body(): pl.pallas_call(functools.partial(sparse_attention_kernel, plane, groups),...  58.7 us
    unnamed x1, local copies, waits for them, and re-layouts  1.57 us

profile of v2, /device:TPU:160, one launch (start us, length us, event | category | flops | bytes accessed | tf_op | source)
XLA Modules:
  0.0 60.3 jit_solution(1788785824260898171)
XLA Ops:
  0.0 58.7 %sparse_attention.1 = bf16[256,256]{1,0:T(8,128)(2,1)} custom-call(s32[2,64]{1,0:T(2,128)} %partner.1, bf16[16,16,256]{2,1,0:T(8,128)(2,1)} %bitcast.3, bf16[16,16,256]{2,1,0:T(8,128)(2,1)} %bitcast.4, bf16[16,16,256]{2,1,0:T(8,128)(2,1)} %bitcast.5), custom_call_target="tpu_custom_call" | custom-call | tf_op jit(solution)/shard_map/sparse_attention/pallas_call | solution.py:410
  58.7 1.6 %copy.6 = bf16[256,256]{1,0:T(8,128)(2,1)} copy(bf16[256,256]{1,0:T(8,128)(2,1)} %sparse_attention.1) | data formatting | bytes 262144

commit v3 on v2

v3 whole, which is shorter than its diff:
```python
import functools
import math

import jax
import jax.numpy as jnp
from jax import lax
from jax.experimental import pallas as pl
from jax.experimental.pallas import tpu as pltpu
from jax.sharding import PartitionSpec as P

DH = 128
BS = 256
SINK_ITERS = 8
SHARPNESS = 2.0
HIGHEST = lax.Precision.HIGHEST
MESH = pl.DeviceIdType.MESH


def bytes_wait(ref, sem):
    pltpu.make_async_copy(ref, ref, sem).wait()


def sparse_attention_kernel(
    plane,
    groups,
    slots,
    partner,
    q_hbm,
    k_hbm,
    v_hbm,
    out,
    crowd,
    qs,
    kv,
    own_a,
    own_b,
    pack_a,
    pack_b,
    slot_a,
    slot_b,
    edge,
    pick,
    part,
    prev,
    col,
    feat,
    partial,
    counts,
    bias,
    top_all,
    den_all,
    mix_all,
    after,
    load_sem,
    col_send,
    col_recv,
    count_send,
    count_recv,
    feat_send,
    feat_recv,
    partial_send,
    partial_recv,
    bias_send,
    bias_recv,
    spread_send,
    spread_recv,
    z_send,
    z_recv,
    edge_send,
    edge_recv,
    back_send,
    back_recv,
    prev_send,
    extra_send,
    prev_recv,
    ready,
):
    own = (own_a, own_b)
    pack = (pack_a, pack_b)
    slot = (slot_a, slot_b)
    s = lax.axis_index("seq")
    g = lax.axis_index("head")
    p = s // plane
    i = s % plane
    base = p * plane
    mirror = (s + plane) % (2 * plane)
    half = plane // 2
    across = plane - base
    slices = 2 * groups
    stride = plane // slices
    inv_scale = 1.0 / math.sqrt(DH)

    def remote(src, dst, ss, rs, seq, head=None):
        return pltpu.make_async_remote_copy(
            src_ref=src,
            dst_ref=dst,
            send_sem=ss,
            recv_sem=rs,
            device_id=(seq, g if head is None else head),
            device_id_type=MESH,
        )

    def signal(sem, seq, head=None):
        pl.semaphore_signal(
            sem,
            inc=1,
            device_id=(seq, g if head is None else head),
            device_id_type=MESH,
        )

    def each_peer(body):
        def wrapped(o, c):
            j = (i + o) % plane
            body(j, base + j)
            return c

        lax.fori_loop(1, plane, wrapped, 0)

    def each_group(body):
        def wrapped(o, c):
            body((g + o) % groups)
            return c

        lax.fori_loop(1, groups, wrapped, 0)

    barrier = pltpu.get_barrier_semaphore()

    @pl.when(p == 0)
    def _():
        for og in range(groups):
            signal(barrier, mirror, og)
        each_group(lambda og: signal(barrier, s, og))

    each_peer(lambda j, d: signal(barrier, d))

    loads = (
        pltpu.make_async_copy(q_hbm, qs, load_sem.at[0]),
        pltpu.make_async_copy(k_hbm, kv.at[pl.ds(0, half)], load_sem.at[1]),
        pltpu.make_async_copy(v_hbm, kv.at[pl.ds(half, half)], load_sem.at[2]),
    )
    for c in loads:
        c.start()
    for c in loads:
        c.wait()
    pooled_q = jnp.sum(jnp.sum(qs[...].astype(jnp.float32), axis=0), axis=0, keepdims=True)
    pooled_k = jnp.sum(
        jnp.sum(kv[pl.ds(0, half)].astype(jnp.float32), axis=0), axis=0, keepdims=True
    )
    for h in range(2):
        lanes = slice(h * DH, (h + 1) * DH)
        col[p, 2 * g + h] = pooled_q[:, lanes] / math.sqrt(BS)
        col[2 + p, 2 * g + h] = pooled_k[:, lanes] / math.sqrt(BS)

    def here(block):
        return (block >= base) & (block < base + plane)

    def tables():
        for h in range(2):
            after[h, plane] = plane
            after[h, plane + 1] = plane

            def link(o, c):
                d = plane - 1 - o
                after[h, d] = jnp.where(here(partner[h, across + d]), d, after[h, d + 1])
                return c

            lax.fori_loop(0, plane, link, 0)

    def count(h):
        def add(d, n):
            return n + jnp.where(here(partner[h, across + d]), 1, 0)

        return lax.fori_loop(0, plane, add, 0)

    def to_column(seq, head):
        rows = pl.ds(2 * g, 2)
        for kind in (p, 2 + p):
            remote(col.at[kind, rows], col.at[kind, rows], col_send, col_recv, seq, head).start()

    bias_copy = remote(bias.at[1], bias.at[0], bias_send, bias_recv, mirror)

    def spread(h):
        lanes = pl.ds(h * DH, DH)
        pltpu.make_async_copy(kv.at[i, :, lanes], own[h].at[i], spread_recv.at[h]).start()
        each_peer(
            lambda j, d: remote(
                kv.at[j, :, lanes], own[h].at[i], spread_send.at[h], spread_recv.at[h], d
            ).start()
        )

    def hand_on():
        @pl.when(i < plane - 1)
        def _():
            for h in range(2):
                lanes = pl.ds(h * DH, DH)
                remote(
                    kv.at[:, :, lanes], prev.at[h], prev_send.at[h], prev_recv.at[h], s + 1
                ).start()

    def exchange(h):
        return remote(pack[h], slot[h], z_send.at[h], z_recv.at[h], mirror)

    def edge_copy(h):
        return remote(own[h].at[plane - 1], edge.at[h], edge_send.at[h], edge_recv.at[h], mirror)

    def spread_done(h):
        bytes_wait(own[h], spread_recv.at[h])

    def fill(h):
        def take(k, at):
            d = after[h, at]
            block = partner[h, across + jnp.minimum(d, plane - 1)]
            pack[h][k] = own[h][jnp.clip(block - base, 0, plane - 1)]
            return d + 1

        lax.fori_loop(0, slots, take, 0)

    def give_back(h):
        bytes_wait(slot[h], z_recv.at[h])

        def choose(j, taken):
            block = partner[h, base + j]
            near = here(block)
            mine = own[h][jnp.clip(block - base, 0, plane - 1)]
            theirs = slot[h][jnp.minimum(taken, slots - 1)]
            pick[h, j] = jnp.where(near, mine, theirs)
            return taken + jnp.where(near, 0, 1)

        lax.fori_loop(0, plane, choose, 0)
        each_peer(
            lambda j, d: remote(
                pick.at[h, j], part.at[h, i], back_send.at[h], back_recv.at[h], d
            ).start()
        )
        pltpu.make_async_copy(pick.at[h, i], part.at[h, i], back_recv.at[h]).start()

        @pl.when(s == plane)
        def _():
            bytes_wait(edge.at[h], edge_recv.at[h])
            pltpu.make_async_copy(edge.at[h], prev.at[h, 0], prev_recv.at[h]).start()

        @pl.when(s > plane)
        def _():
            bytes_wait(edge.at[h], edge_recv.at[h])
            remote(edge.at[h], prev.at[h, i], extra_send.at[h], prev_recv.at[h], base).start()

    def query(h):
        return qs[:, :, h * DH : (h + 1) * DH].reshape(BS, DH)

    def scored(h, key):
        x = lax.dot_general(
            query(h), key, (((1,), (1,)), ((), ())), preferred_element_type=jnp.float32
        )
        return x * inv_scale

    def stacked(ref, h):
        return (
            ref[h, 0:half].reshape(BS, DH),
            ref[h, half:plane].reshape(BS, DH),
        )

    def local():
        for h in range(2):
            lanes = slice(h * DH, (h + 1) * DH)
            x = scored(h, kv[0:half, :, lanes].reshape(BS, DH))
            top = jnp.max(x, axis=1, keepdims=True)
            e = jnp.exp(x - top)
            top_all[h] = top
            den_all[h] = jnp.sum(e, axis=1, keepdims=True)
            mix_all[h] = jnp.dot(
                e.astype(jnp.bfloat16),
                kv[half:plane, :, lanes].reshape(BS, DH),
                preferred_element_type=jnp.float32,
            )

    def merged(h, ref, shift):
        key, val = stacked(ref, h)
        x = scored(h, key)
        if shift is not None:
            x = x + shift
        old = top_all[h]
        top = jnp.maximum(old, jnp.max(x, axis=1, keepdims=True))
        keep = jnp.exp(old - top)
        e = jnp.exp(x - top)
        den = den_all[h] * keep + jnp.sum(e, axis=1, keepdims=True)
        mix = mix_all[h] * keep + jnp.dot(
            e.astype(jnp.bfloat16), val, preferred_element_type=jnp.float32
        )
        return top, den, mix

    def previous(h):
        top, den, mix = merged(h, prev, None)
        top_all[h] = top
        den_all[h] = den
        mix_all[h] = mix

    def early_previous():
        @pl.when(i > 0)
        def _():
            for h in range(2):
                bytes_wait(prev.at[h], prev_recv.at[h])
                previous(h)

    def late_previous(h):
        @pl.when(s == plane)
        def _():
            bytes_wait(prev.at[h], prev_recv.at[h])
            previous(h)

    def finish(h):
        late_previous(h)
        bytes_wait(part.at[h], back_recv.at[h])
        _, den, mix = merged(h, part, bias[0, h : h + 1, 0:1])
        out[:, h * DH : (h + 1) * DH] = (mix * (1.0 / den)).astype(jnp.bfloat16)

    def owned():
        mine = i // stride
        each_peer(
            lambda j, d: remote(
                partial.at[mine], partial.at[mine], partial_send, partial_recv, d
            ).start()
        )

    def scores():
        queries = jnp.concatenate([feat[:, 0, 0, :], feat[:, 1, 0, :]], axis=0)
        keys = jnp.concatenate([feat[:, 2, 0, :], feat[:, 3, 0, :]], axis=0)
        x = lax.dot_general(
            queries,
            keys,
            (((1,), (1,)), ((), ())),
            precision=HIGHEST,
            preferred_element_type=jnp.float32,
        )
        x = x * (SHARPNESS / math.sqrt(2 * DH * groups))
        partial[i // stride, :, 0 : 2 * plane] = x[0:plane]
        partial[i // stride, :, 2 * plane : 4 * plane] = x[plane : 2 * plane]

    def sinkhorn():
        both = jnp.sum(partial[...], axis=0)
        x = jnp.concatenate([both[:, 0 : 2 * plane], both[:, 2 * plane : 4 * plane]], axis=0)

        def sweep(_, x):
            for along in (1, 0):
                top = jnp.max(x, axis=along, keepdims=True)
                x = x - (top + jnp.log(jnp.sum(jnp.exp(x - top), axis=along, keepdims=True)))
            return x

        x = lax.fori_loop(0, SINK_ITERS, sweep, x)
        row = lax.broadcasted_iota(jnp.int32, x.shape, 0)
        col = lax.broadcasted_iota(jnp.int32, x.shape, 1)
        for which, block in ((0, s), (1, mirror)):
            for h in range(2):
                chosen = (row == i + which * plane) & (col == partner[h, block])
                value = jnp.sum(
                    jnp.sum(jnp.where(chosen, x, 0.0), axis=1, keepdims=True), axis=0, keepdims=True
                )
                bias[which, h : h + 1, :] = jnp.broadcast_to(
                    value + math.log(2 * plane), (1, DH)
                )
            bias[which, 2:3, :] = jnp.max(counts[...], axis=0)

    @pl.when(p == 0)
    def _():
        most = jnp.maximum(count(0), count(1))
        counts[g] = jnp.full((1, DH), most, jnp.int32).astype(jnp.float32)
        pl.semaphore_wait(barrier, plane - 1 + groups - 1)
        each_group(lambda og: to_column(s, og))
        each_group(
            lambda og: remote(
                counts.at[g], counts.at[g], count_send, count_recv, s, og
            ).start()
        )
        spread(0)
        spread(1)
        hand_on()
        tables()
        local()
        spread_done(0)
        fill(0)
        pl.semaphore_wait(ready, 1)
        edge_copy(0).start()
        exchange(0).start()
        bytes_wait(feat.at[pl.ds(0, 2 * groups - 1)], col_recv)

        def to_owner(sl, c):
            owner = sl * stride

            @pl.when(owner != i)
            def _():
                remote(col.at[:, sl], feat.at[i], feat_send, feat_recv, base + owner).start()

            @pl.when(owner == i)
            def _():
                pltpu.make_async_copy(col.at[:, sl], feat.at[i], feat_recv).start()

            return c

        lax.fori_loop(0, slices, to_owner, 0)
        spread_done(1)
        fill(1)
        edge_copy(1).start()
        exchange(1).start()

        @pl.when(i % stride == 0)
        def _():
            bytes_wait(feat, feat_recv)
            scores()
            owned()

        early_previous()
        bytes_wait(counts.at[pl.ds(0, groups - 1)], count_recv)

        @pl.when(i % stride == 0)
        def _():
            bytes_wait(partial.at[pl.ds(0, slices - 1)], partial_recv)
            bytes_wait(feat.at[pl.ds(0, slices - 1)], feat_send)

        @pl.when(i % stride != 0)
        def _():
            bytes_wait(partial, partial_recv)
            bytes_wait(feat.at[pl.ds(0, slices)], feat_send)

        sinkhorn()
        crowd[...] = bias[0, 2:3, :]
        bias_copy.start()
        give_back(0)
        finish(0)
        give_back(1)
        finish(1)
        bytes_wait(col.at[pl.ds(0, 2), pl.ds(0, 2 * (groups - 1))], col_send)

        @pl.when(i % stride == 0)
        def _():
            for _ in range(plane - 1):
                bytes_wait(partial.at[0], partial_send)

        bytes_wait(counts.at[pl.ds(0, groups - 1)], count_send)
        for h in range(2):
            edge_copy(h).wait_send()
        bias_copy.wait_send()

    @pl.when(p == 1)
    def _():
        pl.semaphore_wait(barrier, plane - 1 + groups)
        signal(ready, mirror)
        for og in range(groups):
            to_column(mirror, og)
        spread(0)
        spread(1)
        hand_on()
        tables()
        for h in range(2):
            spread_done(h)
            fill(h)
            exchange(h).start()
        local()
        early_previous()
        give_back(0)
        give_back(1)
        bias_copy.wait_recv()
        crowd[...] = bias[0, 2:3, :]
        finish(0)
        finish(1)
        bytes_wait(col.at[pl.ds(0, 2), pl.ds(0, slices)], col_send)

    for h in range(2):
        bytes_wait(own[h].at[pl.ds(0, plane - 1)], spread_send.at[h])
        bytes_wait(pick.at[h, pl.ds(0, plane - 1)], back_send.at[h])
        exchange(h).wait_send()

    @pl.when(i < plane - 1)
    def _():
        for h in range(2):
            bytes_wait(prev.at[h], prev_send.at[h])

    @pl.when(s > plane)
    def _():
        for h in range(2):
            bytes_wait(edge.at[h], extra_send.at[h])


def attention(plane, groups, slots, collective_id, name):
    piece = 2 * BS // plane
    seq = 2 * plane
    half = plane // 2
    width = 2 * DH
    slices = 2 * groups
    dma = pltpu.SemaphoreType.DMA
    hbm = pl.BlockSpec(memory_space=pl.ANY)
    vmem = pl.BlockSpec(memory_space=pltpu.VMEM)
    folded = (half, piece, width)
    one, two = dma(()), dma((2,))
    pieces = pltpu.VMEM((2, plane, piece, DH), jnp.bfloat16)
    head_pieces = pltpu.VMEM((plane, piece, DH), jnp.bfloat16)
    head_slots = pltpu.VMEM((slots, piece, DH), jnp.bfloat16)

    def call(queries, keys, values, partner):
        return pl.pallas_call(
            functools.partial(sparse_attention_kernel, plane, groups, slots),
            out_shape=(
                jax.ShapeDtypeStruct(queries.shape, queries.dtype),
                jax.ShapeDtypeStruct((1, DH), jnp.float32),
            ),
            in_specs=[pl.BlockSpec(memory_space=pltpu.SMEM), hbm, hbm, hbm],
            out_specs=(vmem, vmem),
            scratch_shapes=[
                pltpu.VMEM(folded, jnp.bfloat16),
                pltpu.VMEM((plane, piece, width), jnp.bfloat16),
                head_pieces,
                head_pieces,
                head_slots,
                head_slots,
                head_slots,
                head_slots,
                pltpu.VMEM((2, piece, DH), jnp.bfloat16),
                pieces,
                pieces,
                pieces,
                pltpu.VMEM((4, slices, 1, DH), jnp.float32),
                pltpu.VMEM((plane, 4, 1, DH), jnp.float32),
                pltpu.VMEM((slices, plane, max(DH, 2 * seq)), jnp.float32),
                pltpu.VMEM((groups, 1, DH), jnp.float32),
                pltpu.VMEM((2, 3, DH), jnp.float32),
                pltpu.VMEM((2, BS, 1), jnp.float32),
                pltpu.VMEM((2, BS, 1), jnp.float32),
                pltpu.VMEM((2, BS, DH), jnp.float32),
                pltpu.SMEM((2, plane + 2), jnp.int32),
                dma((3,)),
            ]
            + [one] * 10
            + [two] * 11
            + [pltpu.SemaphoreType.REGULAR],
            compiler_params=pltpu.CompilerParams(
                collective_id=collective_id, has_side_effects=True
            ),
            name=name,
        )(partner, queries.reshape(folded), keys.reshape(folded), values.reshape(folded))

    return call


def solution(mesh):
    seq, groups = mesh.shape["seq"], mesh.shape["head"]
    plane = seq // 2
    whole = attention(plane, groups, plane, 0, "whole")

    def body(queries, keys, values, partner):
        return whole(queries, keys, values, partner)[0]

    return jax.shard_map(
        body,
        mesh=mesh,
        in_specs=(P("seq", "head"), P("seq", "head"), P("seq", "head"), P("head", None)),
        out_specs=P("seq", "head"),
        check_vma=False,
    )
```

time: 60.4 us -> 60.6 us (level)
  the two profiles are of different devices: /device:TPU:160 before, /device:TPU:33 now
where the time goes in v3:
time: 60.6 us; the launch traced here: 60.5 us
  Pallas kernels  58.9 us (97%)
  local copies, waits for them, and re-layouts  1.57 us (3%)
    pallas_call x1, Pallas kernels, call(): pl.pallas_call(functools.partial(sparse_attention_kernel, plane, groups,...  58.9 us
    unnamed x1, local copies, waits for them, and re-layouts  1.57 us

profile of v3, /device:TPU:33, one launch (start us, length us, event | category | flops | bytes accessed | tf_op | source)
XLA Modules:
  0.0 60.5 jit_solution(7610190573859601159)
XLA Ops:
  0.0 58.9 %whole.1 = (bf16[256,256]{1,0:T(8,128)(2,1)}, f32[1,128]{1,0:T(1,128)}) custom-call(s32[2,64]{1,0:T(2,128)} %partner.1, bf16[16,16,256]{2,1,0:T(8,128)(2,1)} %bitcast.3, bf16[16,16,256]{2,1,0:T(8,128)(2,1)} %bitcast.4, bf16[16,16,256]{2,1,0:T(8,128)(2,1)} %bitcast.5), custom_call_target="tpu_custom_call" | custom-call | tf_op jit(solution)/shard_map/whole/pallas_call | solution.py:498
  58.9 1.6 %copy.6 = bf16[256,256]{1,0:T(8,128)(2,1)} copy(bf16[256,256]{1,0:T(8,128)(2,1)} %get-tuple-element.6) | data formatting | bytes 262144

commit v4 on v3

--- a/solution.py
+++ b/solution.py
@@ -12,6 +12,7 @@
 BS = 256
 SINK_ITERS = 8
 SHARPNESS = 2.0
+SLOT_SHARE = 22
 HIGHEST = lax.Precision.HIGHEST
 MESH = pl.DeviceIdType.MESH
 
@@ -424,8 +425,8 @@
         crowd[...] = bias[0, 2:3, :]
         bias_copy.start()
         give_back(0)
+        give_back(1)
         finish(0)
-        give_back(1)
         finish(1)
         bytes_wait(col.at[pl.ds(0, 2), pl.ds(0, 2 * (groups - 1))], col_send)
 
@@ -542,10 +543,17 @@
 def solution(mesh):
     seq, groups = mesh.shape["seq"], mesh.shape["head"]
     plane = seq // 2
-    whole = attention(plane, groups, plane, 0, "whole")
+    slots = plane * SLOT_SHARE // 32
+    packed = attention(plane, groups, slots, 0, "packed")
+    whole = attention(plane, groups, plane, 1, "whole")
 
     def body(queries, keys, values, partner):
-        return whole(queries, keys, values, partner)[0]
+        attended, crowd = packed(queries, keys, values, partner)
+        return lax.cond(
+            crowd[0, 0] > slots,
+            lambda: whole(queries, keys, values, partner)[0],
+            lambda: attended,
+        )
 
     return jax.shard_map(
         body,

time: 60.6 us -> 52.7 us (0.87)
  the two profiles are of different devices: /device:TPU:33 before, /device:TPU:1 now
where the time goes in v4:
time: 52.7 us; the launch traced here: 52.6 us
  Pallas kernels  50.4 us (96%)
  local copies, waits for them, and re-layouts  2.01 us (4%)
    pallas_call x1, Pallas kernels, call(): pl.pallas_call(functools.partial(sparse_attention_kernel, plane, groups,...  50.4 us
    unnamed x11, local copies, waits for them, and re-layouts  2.01 us

profile of v4, /device:TPU:1, one launch (start us, length us, event | category | flops | bytes accessed | tf_op | source)
XLA Modules:
  0.0 52.6 jit_solution(8940651273862299416)
XLA Ops:
  0.0 0.0 copy-start.3
  0.0 0.7 %copy-done.3 = s32[2,64]{1,0:T(2,128)S(1)} copy-done((s32[2,64]{1,0:T(2,128)S(1)}, s32[2,64]{1,0:T(2,128)}, u32[]{:S(2)}) %copy-start.3) | copy-done | bytes 536
  0.7 0.0 copy-start
  0.7 0.0 copy-start.1
  0.7 0.0 copy-start.2
  0.7 50.4 %packed.1 = (bf16[256,256]{1,0:T(8,128)(2,1)S(1)}, f32[1,128]{1,0:T(1,128)}) custom-call(s32[2,64]{1,0:T(2,128)S(1)} %copy-done.3, bf16[16,16,256]{2,1,0:T(8,128)(2,1)} %bitcast.8, bf16[16,16,256]{2,1,0:T(8,128)(2,1)} %bitcast.10, bf16[16,16,256]{2,1,0:T(8,128)(2,1)} %bitcast.12), custom_call_target="tpu_custom_call" | custom-call | tf_op jit(solution)/shard_map/packed/pallas_call | solution.py:499
  51.1 0.0 copy-start.4
  51.2 0.7 %copy-done.4 = f32[1,128]{1,0:T(1,128)S(1)} copy-done((f32[1,128]{1,0:T(1,128)S(1)}, f32[1,128]{1,0:T(1,128)}, u32[]{:S(2)}) %copy-start.4) | copy-done | bytes 536
  51.9 0.0 copy-done
  51.9 0.0 copy-done.1
  51.9 0.0 copy-done.2
  51.9 0.7 %copy.10 = bf16[256,256]{1,0:T(8,128)(2,1)} copy(bf16[256,256]{1,0:T(8,128)(2,1)S(1)} %get-tuple-element.26) | data formatting | bytes 262144
  (1 shorter events, 0.0 us)
Async XLA Ops:
  0.0 0.7 %copy-start.3 = (s32[2,64]{1,0:T(2,128)S(1)}, s32[2,64]{1,0:T(2,128)}, u32[]{:S(2)}) copy-start(s32[2,64]{1,0:T(2,128)} %partner.1) | copy-start | bytes 1540
  0.7 51.2 %copy-start = (bf16[256,256]{1,0:T(8,128)(2,1)S(1)}, bf16[256,256]{1,0:T(8,128)(2,1)}, u32[]{:S(2)}) copy-start(bf16[256,256]{1,0:T(8,128)(2,1)} %param.6) | copy-start | bytes 393220
  0.7 51.2 %copy-start.1 = (bf16[256,256]{1,0:T(8,128)(2,1)S(1)}, bf16[256,256]{1,0:T(8,128)(2,1)}, u32[]{:S(2)}) copy-start(bf16[256,256]{1,0:T(8,128)(2,1)} %param.7) | copy-start | bytes 393220
  0.7 51.2 %copy-start.2 = (bf16[256,256]{1,0:T(8,128)(2,1)S(1)}, bf16[256,256]{1,0:T(8,128)(2,1)}, u32[]{:S(2)}) copy-start(bf16[256,256]{1,0:T(8,128)(2,1)} %param.8) | copy-start | bytes 393220
  51.1 0.7 %copy-start.4 = (f32[1,128]{1,0:T(1,128)S(1)}, f32[1,128]{1,0:T(1,128)}, u32[]{:S(2)}) copy-start(f32[1,128]{1,0:T(1,128)} %get-tuple-element.24) | copy-start | bytes 1540

commit v5 on v4

--- a/solution.py
+++ b/solution.py
@@ -13,8 +13,13 @@
 SINK_ITERS = 8
 SHARPNESS = 2.0
 SLOT_SHARE = 22
+TURNS = ((3, 1), (5, 1), (7, 1), )
 HIGHEST = lax.Precision.HIGHEST
 MESH = pl.DeviceIdType.MESH
+
+
+def farther(at, k):
+    return (at + jnp.where(k == 3, 0, jnp.where(k == 0, 2, 2 * k - 1))) % 4
 
 
 def bytes_wait(ref, sem):
@@ -25,7 +30,7 @@
     plane,
     groups,
     slots,
-    partner,
+    partner_hbm,
     q_hbm,
     k_hbm,
     v_hbm,
@@ -52,6 +57,7 @@
     den_all,
     mix_all,
     after,
+    partner,
     load_sem,
     col_send,
     col_recv,
@@ -75,6 +81,7 @@
     extra_send,
     prev_recv,
     ready,
+    turn,
 ):
     own = (own_a, own_b)
     pack = (pack_a, pack_b)
@@ -111,11 +118,12 @@
 
     def each_peer(body):
         def wrapped(o, c):
-            j = (i + o) % plane
+            j = (farther(i // 8, o // 8) * 4 + farther(i // 2 % 4, o // 2 % 4)) * 2
+            j = j + (i + o + 1) % 2
             body(j, base + j)
             return c
 
-        lax.fori_loop(1, plane, wrapped, 0)
+        lax.fori_loop(0, plane - 1, wrapped, 0)
 
     def each_group(body):
         def wrapped(o, c):
@@ -124,6 +132,7 @@
 
         lax.fori_loop(1, groups, wrapped, 0)
 
+    turns = [(f, l) for f, l in TURNS if f < groups]
     barrier = pltpu.get_barrier_semaphore()
 
     @pl.when(p == 0)
@@ -132,9 +141,16 @@
             signal(barrier, mirror, og)
         each_group(lambda og: signal(barrier, s, og))
 
+    for follower, leader in turns:
+
+        @pl.when((p == 1) & (g == follower))
+        def _():
+            signal(barrier, s, leader)
+
     each_peer(lambda j, d: signal(barrier, d))
 
     loads = (
+        pltpu.make_async_copy(partner_hbm, partner, load_sem.at[3]),
         pltpu.make_async_copy(q_hbm, qs, load_sem.at[0]),
         pltpu.make_async_copy(k_hbm, kv.at[pl.ds(0, half)], load_sem.at[1]),
         pltpu.make_async_copy(v_hbm, kv.at[pl.ds(half, half)], load_sem.at[2]),
@@ -198,8 +214,18 @@
                     kv.at[:, :, lanes], prev.at[h], prev_send.at[h], prev_recv.at[h], s + 1
                 ).start()
 
-    def exchange(h):
-        return remote(pack[h], slot[h], z_send.at[h], z_recv.at[h], mirror)
+    cuts = (0, slots - slots * 5 // 8, slots)
+
+    def exchange(h, part_id):
+        rows = pl.ds(cuts[part_id], cuts[part_id + 1] - cuts[part_id])
+        sems = 2 * h + part_id
+        return remote(
+            pack[h].at[rows], slot[h].at[rows], z_send.at[sems], z_recv.at[sems], mirror
+        )
+
+    def exchange_start(h):
+        exchange(h, 0).start()
+        exchange(h, 1).start()
 
     def edge_copy(h):
         return remote(own[h].at[plane - 1], edge.at[h], edge_send.at[h], edge_recv.at[h], mirror)
@@ -217,7 +243,8 @@
         lax.fori_loop(0, slots, take, 0)
 
     def give_back(h):
-        bytes_wait(slot[h], z_recv.at[h])
+        exchange(h, 0).wait_recv()
+        exchange(h, 1).wait_recv()
 
         def choose(j, taken):
             block = partner[h, base + j]
@@ -379,8 +406,6 @@
         spread_done(0)
         fill(0)
         pl.semaphore_wait(ready, 1)
-        edge_copy(0).start()
-        exchange(0).start()
         bytes_wait(feat.at[pl.ds(0, 2 * groups - 1)], col_recv)
 
         def to_owner(sl, c):
@@ -399,8 +424,6 @@
         lax.fori_loop(0, slices, to_owner, 0)
         spread_done(1)
         fill(1)
-        edge_copy(1).start()
-        exchange(1).start()
 
         @pl.when(i % stride == 0)
         def _():
@@ -408,6 +431,9 @@
             scores()
             owned()
 
+        for h in range(2):
+            edge_copy(h).start()
+            exchange_start(h)
         early_previous()
         bytes_wait(counts.at[pl.ds(0, groups - 1)], count_recv)
 
@@ -438,22 +464,44 @@
         bytes_wait(counts.at[pl.ds(0, groups - 1)], count_send)
         for h in range(2):
             edge_copy(h).wait_send()
+            exchange(h, 0).wait_send()
+            exchange(h, 1).wait_send()
         bias_copy.wait_send()
 
     @pl.when(p == 1)
     def _():
-        pl.semaphore_wait(barrier, plane - 1 + groups)
+        followers = sum(jnp.where(g == leader, 1, 0) for _, leader in turns)
+        pl.semaphore_wait(barrier, plane - 1 + groups + followers)
         signal(ready, mirror)
         for og in range(groups):
             to_column(mirror, og)
         spread(0)
         spread(1)
+        tables()
+        spread_done(0)
+        fill(0)
+
+        for follower, _ in turns:
+
+            @pl.when(g == follower)
+            def _():
+                pl.semaphore_wait(turn, 1)
+
+        exchange_start(0)
+        spread_done(1)
+        fill(1)
+        exchange_start(1)
         hand_on()
-        tables()
-        for h in range(2):
-            spread_done(h)
-            fill(h)
-            exchange(h).start()
+        exchange(0, 0).wait_send()
+        exchange(0, 1).wait_send()
+        exchange(1, 0).wait_send()
+
+        for follower, leader in turns:
+
+            @pl.when(g == leader)
+            def _():
+                signal(turn, s, follower)
+
         local()
         early_previous()
         give_back(0)
@@ -462,12 +510,12 @@
         crowd[...] = bias[0, 2:3, :]
         finish(0)
         finish(1)
+        exchange(1, 1).wait_send()
         bytes_wait(col.at[pl.ds(0, 2), pl.ds(0, slices)], col_send)
 
     for h in range(2):
         bytes_wait(own[h].at[pl.ds(0, plane - 1)], spread_send.at[h])
         bytes_wait(pick.at[h, pl.ds(0, plane - 1)], back_send.at[h])
-        exchange(h).wait_send()
 
     @pl.when(i < plane - 1)
     def _():
@@ -500,9 +548,9 @@
             functools.partial(sparse_attention_kernel, plane, groups, slots),
             out_shape=(
                 jax.ShapeDtypeStruct(queries.shape, queries.dtype),
-                jax.ShapeDtypeStruct((1, DH), jnp.float32),
+                pltpu.VMEM((1, DH), jnp.float32),
             ),
-            in_specs=[pl.BlockSpec(memory_space=pltpu.SMEM), hbm, hbm, hbm],
+            in_specs=[pl.BlockSpec(memory_space=pltpu.HBM), hbm, hbm, hbm],
             out_specs=(vmem, vmem),
             scratch_shapes=[
                 pltpu.VMEM(folded, jnp.bfloat16),
@@ -526,11 +574,14 @@
                 pltpu.VMEM((2, BS, 1), jnp.float32),
                 pltpu.VMEM((2, BS, DH), jnp.float32),
                 pltpu.SMEM((2, plane + 2), jnp.int32),
-                dma((3,)),
+                pltpu.SMEM((2, seq), jnp.int32),
+                dma((4,)),
             ]
             + [one] * 10
-            + [two] * 11
-            + [pltpu.SemaphoreType.REGULAR],
+            + [two] * 2
+            + [dma((4,))] * 2
+            + [two] * 7
+            + [pltpu.SemaphoreType.REGULAR] * 2,
             compiler_params=pltpu.CompilerParams(
                 collective_id=collective_id, has_side_effects=True
             ),

time: 52.7 us -> 49.2 us (0.934)
  the two profiles are of different devices: /device:TPU:1 before, /device:TPU:160 now
where the time goes in v5:
time: 49.2 us; the launch traced here: 49.1 us
  Pallas kernels  47.7 us (97%)
  local copies, waits for them, and re-layouts  1.35 us (3%)
    pallas_call x1, Pallas kernels, call(): pl.pallas_call(functools.partial(sparse_attention_kernel, plane, groups,...  47.7 us
    unnamed x9, local copies, waits for them, and re-layouts  1.35 us

profile of v5, /device:TPU:160, one launch (start us, length us, event | category | flops | bytes accessed | tf_op | source)
XLA Modules:
  0.0 49.1 jit_solution(7884668288247724595)
XLA Ops:
  0.0 0.0 copy-start.3
  0.0 0.7 %copy-done.3 = s32[2,64]{1,0:T(2,128)S(1)} copy-done((s32[2,64]{1,0:T(2,128)S(1)}, s32[2,64]{1,0:T(2,128)}, u32[]{:S(2)}) %copy-start.3) | copy-done | bytes 536
  0.7 0.0 copy-start
  0.7 0.0 copy-start.1
  0.7 0.0 copy-start.2
  0.7 47.7 %packed.1 = (bf16[256,256]{1,0:T(8,128)(2,1)S(1)}, f32[1,128]{1,0:T(1,128)S(1)}) custom-call(s32[2,64]{1,0:T(2,128)S(1)} %copy-done.3, bf16[16,16,256]{2,1,0:T(8,128)(2,1)} %bitcast.9, bf16[16,16,256]{2,1,0:T(8,128)(2,1)} %bitcast.11, bf16[16,16,256]{2,1,0:T(8,128)(2,1)} %bitcast.13), custom_call_target="tpu_custom_call" | custom-call | tf_op jit(solution)/shard_map/packed/pallas_call | solution.py:547
  48.4 0.0 copy-done
  48.4 0.0 copy-done.1
  48.4 0.0 copy-done.2
  48.4 0.7 %copy.10 = bf16[256,256]{1,0:T(8,128)(2,1)} copy(bf16[256,256]{1,0:T(8,128)(2,1)S(1)} %get-tuple-element.26) | data formatting | bytes 262144
  (1 shorter events, 0.0 us)
Async XLA Ops:
  0.0 0.7 %copy-start.3 = (s32[2,64]{1,0:T(2,128)S(1)}, s32[2,64]{1,0:T(2,128)}, u32[]{:S(2)}) copy-start(s32[2,64]{1,0:T(2,128)} %partner_hbm.1) | copy-start | bytes 1540
  0.7 47.7 %copy-start = (bf16[256,256]{1,0:T(8,128)(2,1)S(1)}, bf16[256,256]{1,0:T(8,128)(2,1)}, u32[]{:S(2)}) copy-start(bf16[256,256]{1,0:T(8,128)(2,1)} %param.6) | copy-start | bytes 393220
  0.7 47.7 %copy-start.1 = (bf16[256,256]{1,0:T(8,128)(2,1)S(1)}, bf16[256,256]{1,0:T(8,128)(2,1)}, u32[]{:S(2)}) copy-start(bf16[256,256]{1,0:T(8,128)(2,1)} %param.7) | copy-start | bytes 393220
  0.7 47.7 %copy-start.2 = (bf16[256,256]{1,0:T(8,128)(2,1)S(1)}, bf16[256,256]{1,0:T(8,128)(2,1)}, u32[]{:S(2)}) copy-start(bf16[256,256]{1,0:T(8,128)(2,1)} %param.8) | copy-start | bytes 393220

commit v6 on v5

--- a/solution.py
+++ b/solution.py
@@ -12,14 +12,14 @@
 BS = 256
 SINK_ITERS = 8
 SHARPNESS = 2.0
-SLOT_SHARE = 22
+SLOT_SHARE = 40
 TURNS = ((3, 1), (5, 1), (7, 1), )
 HIGHEST = lax.Precision.HIGHEST
 MESH = pl.DeviceIdType.MESH
 
 
-def farther(at, k):
-    return (at + jnp.where(k == 3, 0, jnp.where(k == 0, 2, 2 * k - 1))) % 4
+def far_first(size):
+    return sorted(range(size), key=lambda o: (min(o, size - o) == 0, -min(o, size - o)))
 
 
 def bytes_wait(ref, sem):
@@ -38,12 +38,9 @@
     crowd,
     qs,
     kv,
-    own_a,
-    own_b,
-    pack_a,
-    pack_b,
-    slot_a,
-    slot_b,
+    own,
+    pack,
+    slot,
     edge,
     pick,
     part,
@@ -83,9 +80,6 @@
     ready,
     turn,
 ):
-    own = (own_a, own_b)
-    pack = (pack_a, pack_b)
-    slot = (slot_a, slot_b)
     s = lax.axis_index("seq")
     g = lax.axis_index("head")
     p = s // plane
@@ -116,14 +110,33 @@
             device_id_type=MESH,
         )
 
+    x_size = 4 if plane % 8 == 0 else 1
+    y_size = plane // (2 * x_size)
+    x_at, y_at = i // (2 * y_size), i // 2 % y_size
+    y_order = [(y_at + o) % y_size * 2 for o in far_first(y_size)]
+    cores = [1 - i % 2, i % 2]
+
     def each_peer(body):
-        def wrapped(o, c):
-            j = (farther(i // 8, o // 8) * 4 + farther(i // 2 % 4, o // 2 % 4)) * 2
-            j = j + (i + o + 1) % 2
-            body(j, base + j)
-            return c
-
-        lax.fori_loop(0, plane - 1, wrapped, 0)
+        def line(k, carry):
+            o = 0
+            for at, offset in enumerate(far_first(x_size)):
+                o = jnp.where(k == at, offset, o)
+            x = (x_at + o) % x_size * (2 * y_size)
+            near = None
+            for y in y_order:
+                for core in cores:
+                    near = x + y + core
+                    if y is y_order[-1] and core is cores[-1]:
+                        break
+                    body(near, base + near)
+
+            @pl.when(k < x_size - 1)
+            def _():
+                body(near, base + near)
+
+            return carry
+
+        lax.fori_loop(0, x_size, line, 0)
 
     def each_group(body):
         def wrapped(o, c):
@@ -171,23 +184,28 @@
     def here(block):
         return (block >= base) & (block < base + plane)
 
+    both = 2 * plane
+
+    def wants(c, side):
+        h = jnp.where(c >= plane, 1, 0)
+        return partner[h, side + c - h * plane]
+
     def tables():
-        for h in range(2):
-            after[h, plane] = plane
-            after[h, plane + 1] = plane
-
-            def link(o, c):
-                d = plane - 1 - o
-                after[h, d] = jnp.where(here(partner[h, across + d]), d, after[h, d + 1])
-                return c
-
-            lax.fori_loop(0, plane, link, 0)
-
-    def count(h):
-        def add(d, n):
-            return n + jnp.where(here(partner[h, across + d]), 1, 0)
-
-        return lax.fori_loop(0, plane, add, 0)
+        after[both] = both
+        after[both + 1] = both
+
+        def link(o, carry):
+            c = both - 1 - o
+            after[c] = jnp.where(here(wants(c, across)), c, after[c + 1])
+            return carry
+
+        lax.fori_loop(0, both, link, 0)
+
+    def count(first, last, side, near):
+        def add(c, n):
+            return n + jnp.where(here(wants(c, side)) == near, 1, 0)
+
+        return lax.fori_loop(first, last, add, 0)
 
     def to_column(seq, head):
         rows = pl.ds(2 * g, 2)
@@ -196,81 +214,70 @@
 
     bias_copy = remote(bias.at[1], bias.at[0], bias_send, bias_recv, mirror)
 
-    def spread(h):
-        lanes = pl.ds(h * DH, DH)
-        pltpu.make_async_copy(kv.at[i, :, lanes], own[h].at[i], spread_recv.at[h]).start()
+    def spread():
+        pltpu.make_async_copy(kv.at[i], own.at[i], spread_recv).start()
         each_peer(
-            lambda j, d: remote(
-                kv.at[j, :, lanes], own[h].at[i], spread_send.at[h], spread_recv.at[h], d
-            ).start()
+            lambda j, d: remote(kv.at[j], own.at[i], spread_send, spread_recv, d).start()
         )
 
     def hand_on():
         @pl.when(i < plane - 1)
         def _():
+            remote(kv, prev, prev_send, prev_recv, s + 1).start()
+
+    cuts = (0, slots - slots // 3, slots)
+
+    def exchange(part_id):
+        rows = pl.ds(cuts[part_id], cuts[part_id + 1] - cuts[part_id])
+        return remote(
+            pack.at[rows], slot.at[rows], z_send.at[part_id], z_recv.at[part_id], mirror
+        )
+
+    edge_copy = remote(own.at[plane - 1], edge, edge_send, edge_recv, mirror)
+
+    def fill():
+        bytes_wait(own, spread_recv)
+
+        def take(k, at):
+            c = after[at]
+            block = wants(jnp.minimum(c, both - 1), across)
+            piece = jnp.clip(block - base, 0, plane - 1)
+            pack[k] = jnp.where(c < plane, own[piece, :, 0:DH], own[piece, :, DH : 2 * DH])
+            return c + 1
+
+        lax.fori_loop(0, slots, take, 0)
+
+    def give_back():
+        exchange(0).wait_recv()
+        exchange(1).wait_recv()
+
+        def choose(j, taken):
+            later = []
             for h in range(2):
-                lanes = pl.ds(h * DH, DH)
-                remote(
-                    kv.at[:, :, lanes], prev.at[h], prev_send.at[h], prev_recv.at[h], s + 1
-                ).start()
-
-    cuts = (0, slots - slots * 5 // 8, slots)
-
-    def exchange(h, part_id):
-        rows = pl.ds(cuts[part_id], cuts[part_id + 1] - cuts[part_id])
-        sems = 2 * h + part_id
-        return remote(
-            pack[h].at[rows], slot[h].at[rows], z_send.at[sems], z_recv.at[sems], mirror
-        )
-
-    def exchange_start(h):
-        exchange(h, 0).start()
-        exchange(h, 1).start()
-
-    def edge_copy(h):
-        return remote(own[h].at[plane - 1], edge.at[h], edge_send.at[h], edge_recv.at[h], mirror)
-
-    def spread_done(h):
-        bytes_wait(own[h], spread_recv.at[h])
-
-    def fill(h):
-        def take(k, at):
-            d = after[h, at]
-            block = partner[h, across + jnp.minimum(d, plane - 1)]
-            pack[h][k] = own[h][jnp.clip(block - base, 0, plane - 1)]
-            return d + 1
-
-        lax.fori_loop(0, slots, take, 0)
-
-    def give_back(h):
-        exchange(h, 0).wait_recv()
-        exchange(h, 1).wait_recv()
-
-        def choose(j, taken):
-            block = partner[h, base + j]
-            near = here(block)
-            mine = own[h][jnp.clip(block - base, 0, plane - 1)]
-            theirs = slot[h][jnp.minimum(taken, slots - 1)]
-            pick[h, j] = jnp.where(near, mine, theirs)
-            return taken + jnp.where(near, 0, 1)
-
-        lax.fori_loop(0, plane, choose, 0)
+                lanes = slice(h * DH, (h + 1) * DH)
+                block = partner[h, base + j]
+                near = here(block)
+                mine = own[jnp.clip(block - base, 0, plane - 1), :, lanes]
+                theirs = slot[jnp.minimum(taken[h], slots - 1)]
+                pick[j, :, lanes] = jnp.where(near, mine, theirs)
+                later.append(taken[h] + jnp.where(near, 0, 1))
+            return tuple(later)
+
+        lax.fori_loop(0, plane, choose, (jnp.int32(0), count(0, plane, base, False)))
         each_peer(
-            lambda j, d: remote(
-                pick.at[h, j], part.at[h, i], back_send.at[h], back_recv.at[h], d
-            ).start()
-        )
-        pltpu.make_async_copy(pick.at[h, i], part.at[h, i], back_recv.at[h]).start()
+            lambda j, d: remote(pick.at[j], part.at[i], back_send, back_recv, d).start()
+        )
+        pltpu.make_async_copy(pick.at[i], part.at[i], back_recv).start()
 
         @pl.when(s == plane)
         def _():
-            bytes_wait(edge.at[h], edge_recv.at[h])
-            pltpu.make_async_copy(edge.at[h], prev.at[h, 0], prev_recv.at[h]).start()
+            bytes_wait(edge, edge_recv)
+            pltpu.make_async_copy(edge, prev.at[0], prev_recv).start()
 
         @pl.when(s > plane)
         def _():
-            bytes_wait(edge.at[h], edge_recv.at[h])
-            remote(edge.at[h], prev.at[h, i], extra_send.at[h], prev_recv.at[h], base).start()
+            bytes_wait(edge, edge_recv)
+            remote(edge, prev.at[i], extra_send, prev_recv, base).start()
 
     def query(h):
         return qs[:, :, h * DH : (h + 1) * DH].reshape(BS, DH)
@@ -282,9 +289,10 @@
         return x * inv_scale
 
     def stacked(ref, h):
+        lanes = slice(h * DH, (h + 1) * DH)
         return (
-            ref[h, 0:half].reshape(BS, DH),
-            ref[h, half:plane].reshape(BS, DH),
+            ref[0:half, :, lanes].reshape(BS, DH),
+            ref[half:plane, :, lanes].reshape(BS, DH),
         )
 
     def local():
@@ -325,21 +333,23 @@
     def early_previous():
         @pl.when(i > 0)
         def _():
+            bytes_wait(prev, prev_recv)
             for h in range(2):
-                bytes_wait(prev.at[h], prev_recv.at[h])
                 previous(h)
 
-    def late_previous(h):
+    def late_previous():
         @pl.when(s == plane)
         def _():
-            bytes_wait(prev.at[h], prev_recv.at[h])
-            previous(h)
-
-    def finish(h):
-        late_previous(h)
-        bytes_wait(part.at[h], back_recv.at[h])
-        _, den, mix = merged(h, part, bias[0, h : h + 1, 0:1])
-        out[:, h * DH : (h + 1) * DH] = (mix * (1.0 / den)).astype(jnp.bfloat16)
+            bytes_wait(prev, prev_recv)
+            for h in range(2):
+                previous(h)
+
+    def finish():
+        late_previous()
+        bytes_wait(part, back_recv)
+        for h in range(2):
+            _, den, mix = merged(h, part, bias[0, h : h + 1, 0:1])
+            out[:, h * DH : (h + 1) * DH] = (mix * (1.0 / den)).astype(jnp.bfloat16)
 
     def owned():
         mine = i // stride
@@ -389,8 +399,8 @@
 
     @pl.when(p == 0)
     def _():
-        most = jnp.maximum(count(0), count(1))
-        counts[g] = jnp.full((1, DH), most, jnp.int32).astype(jnp.float32)
+        crossing = count(0, both, across, True)
+        counts[g] = jnp.full((1, DH), crossing, jnp.int32).astype(jnp.float32)
         pl.semaphore_wait(barrier, plane - 1 + groups - 1)
         each_group(lambda og: to_column(s, og))
         each_group(
@@ -398,13 +408,11 @@
                 counts.at[g], counts.at[g], count_send, count_recv, s, og
             ).start()
         )
-        spread(0)
-        spread(1)
+        spread()
         hand_on()
         tables()
         local()
-        spread_done(0)
-        fill(0)
+        fill()
         pl.semaphore_wait(ready, 1)
         bytes_wait(feat.at[pl.ds(0, 2 * groups - 1)], col_recv)
 
@@ -422,8 +430,6 @@
             return c
 
         lax.fori_loop(0, slices, to_owner, 0)
-        spread_done(1)
-        fill(1)
 
         @pl.when(i % stride == 0)
         def _():
@@ -431,9 +437,9 @@
             scores()
             owned()
 
-        for h in range(2):
-            edge_copy(h).start()
-            exchange_start(h)
+        edge_copy.start()
+        exchange(0).start()
+        exchange(1).start()
         early_previous()
         bytes_wait(counts.at[pl.ds(0, groups - 1)], count_recv)
 
@@ -450,10 +456,8 @@
         sinkhorn()
         crowd[...] = bias[0, 2:3, :]
         bias_copy.start()
-        give_back(0)
-        give_back(1)
-        finish(0)
-        finish(1)
+        give_back()
+        finish()
         bytes_wait(col.at[pl.ds(0, 2), pl.ds(0, 2 * (groups - 1))], col_send)
 
         @pl.when(i % stride == 0)
@@ -462,10 +466,9 @@
                 bytes_wait(partial.at[0], partial_send)
 
         bytes_wait(counts.at[pl.ds(0, groups - 1)], count_send)
-        for h in range(2):
-            edge_copy(h).wait_send()
-            exchange(h, 0).wait_send()
-            exchange(h, 1).wait_send()
+        edge_copy.wait_send()
+        exchange(0).wait_send()
+        exchange(1).wait_send()
         bias_copy.wait_send()
 
     @pl.when(p == 1)
@@ -475,11 +478,9 @@
         signal(ready, mirror)
         for og in range(groups):
             to_column(mirror, og)
-        spread(0)
-        spread(1)
+        spread()
         tables()
-        spread_done(0)
-        fill(0)
+        fill()
 
         for follower, _ in turns:
 
@@ -487,14 +488,10 @@
             def _():
                 pl.semaphore_wait(turn, 1)
 
-        exchange_start(0)
-        spread_done(1)
-        fill(1)
-        exchange_start(1)
+        exchange(0).start()
+        exchange(1).start()
         hand_on()
-        exchange(0, 0).wait_send()
-        exchange(0, 1).wait_send()
-        exchange(1, 0).wait_send()
+        exchange(0).wait_send()
 
         for follower, leader in turns:
 
@@ -504,28 +501,23 @@
 
         local()
         early_previous()
-        give_back(0)
-        give_back(1)
+        give_back()
         bias_copy.wait_recv()
         crowd[...] = bias[0, 2:3, :]
-        finish(0)
-        finish(1)
-        exchange(1, 1).wait_send()
+        finish()
+        exchange(1).wait_send()
         bytes_wait(col.at[pl.ds(0, 2), pl.ds(0, slices)], col_send)
 
-    for h in range(2):
-        bytes_wait(own[h].at[pl.ds(0, plane - 1)], spread_send.at[h])
-        bytes_wait(pick.at[h, pl.ds(0, plane - 1)], back_send.at[h])
+    bytes_wait(own.at[pl.ds(0, plane - 1)], spread_send)
+    bytes_wait(pick.at[pl.ds(0, plane - 1)], back_send)
 
     @pl.when(i < plane - 1)
     def _():
-        for h in range(2):
-            bytes_wait(prev.at[h], prev_send.at[h])
+        bytes_wait(prev, prev_send)
 
     @pl.when(s > plane)
     def _():
-        for h in range(2):
-            bytes_wait(edge.at[h], extra_send.at[h])
+        bytes_wait(edge, extra_send)
 
 
 def attention(plane, groups, slots, collective_id, name):
@@ -539,8 +531,7 @@
     vmem = pl.BlockSpec(memory_space=pltpu.VMEM)
     folded = (half, piece, width)
     one, two = dma(()), dma((2,))
-    pieces = pltpu.VMEM((2, plane, piece, DH), jnp.bfloat16)
-    head_pieces = pltpu.VMEM((plane, piece, DH), jnp.bfloat16)
+    pieces = pltpu.VMEM((plane, piece, width), jnp.bfloat16)
     head_slots = pltpu.VMEM((slots, piece, DH), jnp.bfloat16)
 
     def call(queries, keys, values, partner):
@@ -554,14 +545,11 @@
             out_specs=(vmem, vmem),
             scratch_shapes=[
                 pltpu.VMEM(folded, jnp.bfloat16),
-                pltpu.VMEM((plane, piece, width), jnp.bfloat16),
-                head_pieces,
-                head_pieces,
+                pieces,
+                pieces,
                 head_slots,
                 head_slots,
-                head_slots,
-                head_slots,
-                pltpu.VMEM((2, piece, DH), jnp.bfloat16),
+                pltpu.VMEM((piece, width), jnp.bfloat16),
                 pieces,
                 pieces,
                 pieces,
@@ -573,14 +561,13 @@
                 pltpu.VMEM((2, BS, 1), jnp.float32),
                 pltpu.VMEM((2, BS, 1), jnp.float32),
                 pltpu.VMEM((2, BS, DH), jnp.float32),
-                pltpu.SMEM((2, plane + 2), jnp.int32),
+                pltpu.SMEM((seq + 2,), jnp.int32),
                 pltpu.SMEM((2, seq), jnp.int32),
                 dma((4,)),
             ]
-            + [one] * 10
+            + [one] * 12
             + [two] * 2
-            + [dma((4,))] * 2
-            + [two] * 7
+            + [one] * 7
             + [pltpu.SemaphoreType.REGULAR] * 2,
             compiler_params=pltpu.CompilerParams(
                 collective_id=collective_id, has_side_effects=True
@@ -594,9 +581,9 @@
 def solution(mesh):
     seq, groups = mesh.shape["seq"], mesh.shape["head"]
     plane = seq // 2
-    slots = plane * SLOT_SHARE // 32
+    slots = seq * SLOT_SHARE // 64
     packed = attention(plane, groups, slots, 0, "packed")
-    whole = attention(plane, groups, plane, 1, "whole")
+    whole = attention(plane, groups, seq, 1, "whole")
 
     def body(queries, keys, values, partner):
         attended, crowd = packed(queries, keys, values, partner)

time: 49.2 us -> 51.4 us (1.045)
  the two profiles are of different devices: /device:TPU:160 before, /device:TPU:1 now
where the time goes in v6:
time: 51.4 us; the launch traced here: 51.3 us
  Pallas kernels  49.9 us (97%)
  local copies, waits for them, and re-layouts  1.35 us (3%)
    pallas_call x1, Pallas kernels, call(): pl.pallas_call(functools.partial(sparse_attention_kernel, plane, groups,...  49.9 us
    unnamed x9, local copies, waits for them, and re-layouts  1.35 us

profile of v6, /device:TPU:1, one launch (start us, length us, event | category | flops | bytes accessed | tf_op | source)
XLA Modules:
  0.0 51.3 jit_solution(8237271327791128073)
XLA Ops:
  0.0 0.0 copy-start.3
  0.0 0.7 %copy-done.3 = s32[2,64]{1,0:T(2,128)S(1)} copy-done((s32[2,64]{1,0:T(2,128)S(1)}, s32[2,64]{1,0:T(2,128)}, u32[]{:S(2)}) %copy-start.3) | copy-done | bytes 536
  0.7 0.0 copy-start
  0.7 0.0 copy-start.1
  0.7 0.0 copy-start.2
  0.7 49.9 %packed.1 = (bf16[256,256]{1,0:T(8,128)(2,1)S(1)}, f32[1,128]{1,0:T(1,128)S(1)}) custom-call(s32[2,64]{1,0:T(2,128)S(1)} %copy-done.3, bf16[16,16,256]{2,1,0:T(8,128)(2,1)} %bitcast.9, bf16[16,16,256]{2,1,0:T(8,128)(2,1)} %bitcast.11, bf16[16,16,256]{2,1,0:T(8,128)(2,1)} %bitcast.13), custom_call_target="tpu_custom_call" | custom-call | tf_op jit(solution)/shard_map/packed/pallas_call | solution.py:538
  50.6 0.0 copy-done
  50.6 0.0 copy-done.1
  50.6 0.0 copy-done.2
  50.6 0.7 %copy.10 = bf16[256,256]{1,0:T(8,128)(2,1)} copy(bf16[256,256]{1,0:T(8,128)(2,1)S(1)} %get-tuple-element.26) | data formatting | bytes 262144
  (1 shorter events, 0.0 us)
Async XLA Ops:
  0.0 0.7 %copy-start.3 = (s32[2,64]{1,0:T(2,128)S(1)}, s32[2,64]{1,0:T(2,128)}, u32[]{:S(2)}) copy-start(s32[2,64]{1,0:T(2,128)} %partner_hbm.1) | copy-start | bytes 1540
  0.7 49.9 %copy-start = (bf16[256,256]{1,0:T(8,128)(2,1)S(1)}, bf16[256,256]{1,0:T(8,128)(2,1)}, u32[]{:S(2)}) copy-start(bf16[256,256]{1,0:T(8,128)(2,1)} %param.6) | copy-start | bytes 393220
  0.7 49.9 %copy-start.1 = (bf16[256,256]{1,0:T(8,128)(2,1)S(1)}, bf16[256,256]{1,0:T(8,128)(2,1)}, u32[]{:S(2)}) copy-start(bf16[256,256]{1,0:T(8,128)(2,1)} %param.7) | copy-start | bytes 393220
  0.7 49.9 %copy-start.2 = (bf16[256,256]{1,0:T(8,128)(2,1)S(1)}, bf16[256,256]{1,0:T(8,128)(2,1)}, u32[]{:S(2)}) copy-start(bf16[256,256]{1,0:T(8,128)(2,1)} %param.8) | copy-start | bytes 393220

commit v7 on v5

--- a/solution.py
+++ b/solution.py
@@ -18,8 +18,8 @@
 MESH = pl.DeviceIdType.MESH
 
 
-def farther(at, k):
-    return (at + jnp.where(k == 3, 0, jnp.where(k == 0, 2, 2 * k - 1))) % 4
+def far_first(size):
+    return sorted(range(size), key=lambda o: (min(o, size - o) == 0, -min(o, size - o)))
 
 
 def bytes_wait(ref, sem):
@@ -116,14 +116,33 @@
             device_id_type=MESH,
         )
 
+    x_size = 4 if plane % 8 == 0 else 1
+    y_size = plane // (2 * x_size)
+    x_at, y_at = i // (2 * y_size), i // 2 % y_size
+    y_order = [(y_at + o) % y_size * 2 for o in far_first(y_size)]
+    cores = [1 - i % 2, i % 2]
+
     def each_peer(body):
-        def wrapped(o, c):
-            j = (farther(i // 8, o // 8) * 4 + farther(i // 2 % 4, o // 2 % 4)) * 2
-            j = j + (i + o + 1) % 2
-            body(j, base + j)
-            return c
-
-        lax.fori_loop(0, plane - 1, wrapped, 0)
+        def line(k, carry):
+            o = 0
+            for at, offset in enumerate(far_first(x_size)):
+                o = jnp.where(k == at, offset, o)
+            x = (x_at + o) % x_size * (2 * y_size)
+            near = None
+            for y in y_order:
+                for core in cores:
+                    near = x + y + core
+                    if y is y_order[-1] and core is cores[-1]:
+                        break
+                    body(near, base + near)
+
+            @pl.when(k < x_size - 1)
+            def _():
+                body(near, base + near)
+
+            return carry
+
+        lax.fori_loop(0, x_size, line, 0)
 
     def each_group(body):
         def wrapped(o, c):
@@ -494,13 +513,13 @@
         hand_on()
         exchange(0, 0).wait_send()
         exchange(0, 1).wait_send()
-        exchange(1, 0).wait_send()
-
         for follower, leader in turns:
 
             @pl.when(g == leader)
             def _():
                 signal(turn, s, follower)
+
+        exchange(1, 0).wait_send()
 
         local()
         early_previous()

time: 49.2 us -> 48.5 us (0.986)
  the two profiles are of different devices: /device:TPU:160 before, /device:TPU:161 now
where the time goes in v7:
time: 48.5 us; the launch traced here: 48.3 us
  Pallas kernels  46.9 us (97%)
  local copies, waits for them, and re-layouts  1.35 us (3%)
    pallas_call x1, Pallas kernels, call(): pl.pallas_call(functools.partial(sparse_attention_kernel, plane, groups,...  46.9 us
    unnamed x9, local copies, waits for them, and re-layouts  1.35 us

profile of v7, /device:TPU:161, one launch (start us, length us, event | category | flops | bytes accessed | tf_op | source)
XLA Modules:
  0.0 48.3 jit_solution(3948314294342850928)
XLA Ops:
  0.0 0.0 copy-start.3
  0.0 0.7 %copy-done.3 = s32[2,64]{1,0:T(2,128)S(1)} copy-done((s32[2,64]{1,0:T(2,128)S(1)}, s32[2,64]{1,0:T(2,128)}, u32[]{:S(2)}) %copy-start.3) | copy-done | bytes 536
  0.7 0.0 copy-start
  0.7 0.0 copy-start.1
  0.7 0.0 copy-start.2
  0.7 46.9 %packed.1 = (bf16[256,256]{1,0:T(8,128)(2,1)S(1)}, f32[1,128]{1,0:T(1,128)S(1)}) custom-call(s32[2,64]{1,0:T(2,128)S(1)} %copy-done.3, bf16[16,16,256]{2,1,0:T(8,128)(2,1)} %bitcast.9, bf16[16,16,256]{2,1,0:T(8,128)(2,1)} %bitcast.11, bf16[16,16,256]{2,1,0:T(8,128)(2,1)} %bitcast.13), custom_call_target="tpu_custom_call" | custom-call | tf_op jit(solution)/shard_map/packed/pallas_call | solution.py:566
  47.6 0.0 copy-done
  47.7 0.0 copy-done.1
  47.7 0.0 copy-done.2
  47.7 0.7 %copy.10 = bf16[256,256]{1,0:T(8,128)(2,1)} copy(bf16[256,256]{1,0:T(8,128)(2,1)S(1)} %get-tuple-element.26) | data formatting | bytes 262144
  (1 shorter events, 0.0 us)
Async XLA Ops:
  0.0 0.7 %copy-start.3 = (s32[2,64]{1,0:T(2,128)S(1)}, s32[2,64]{1,0:T(2,128)}, u32[]{:S(2)}) copy-start(s32[2,64]{1,0:T(2,128)} %partner_hbm.1) | copy-start | bytes 1540
  0.7 47.0 %copy-start = (bf16[256,256]{1,0:T(8,128)(2,1)S(1)}, bf16[256,256]{1,0:T(8,128)(2,1)}, u32[]{:S(2)}) copy-start(bf16[256,256]{1,0:T(8,128)(2,1)} %param.6) | copy-start | bytes 393220
  0.7 47.0 %copy-start.1 = (bf16[256,256]{1,0:T(8,128)(2,1)S(1)}, bf16[256,256]{1,0:T(8,128)(2,1)}, u32[]{:S(2)}) copy-start(bf16[256,256]{1,0:T(8,128)(2,1)} %param.7) | copy-start | bytes 393220
  0.7 47.0 %copy-start.2 = (bf16[256,256]{1,0:T(8,128)(2,1)S(1)}, bf16[256,256]{1,0:T(8,128)(2,1)}, u32[]{:S(2)}) copy-start(bf16[256,256]{1,0:T(8,128)(2,1)} %param.8) | copy-start | bytes 393220

commit v8 on v7

--- a/solution.py
+++ b/solution.py
@@ -13,7 +13,7 @@
 SINK_ITERS = 8
 SHARPNESS = 2.0
 SLOT_SHARE = 22
-TURNS = ((3, 1), (5, 1), (7, 1), )
+TURNS = ((3, 1), (5, 1), (7, 5))
 HIGHEST = lax.Precision.HIGHEST
 MESH = pl.DeviceIdType.MESH
 

time: 48.5 us -> 47.6 us (0.981)
  the two profiles are of different devices: /device:TPU:161 before, /device:TPU:225 now
where the time goes in v8:
time: 47.6 us; the launch traced here: 47.4 us
  Pallas kernels  46 us (97%)
  local copies, waits for them, and re-layouts  1.35 us (3%)
    pallas_call x1, Pallas kernels, call(): pl.pallas_call(functools.partial(sparse_attention_kernel, plane, groups,...  46 us
    unnamed x9, local copies, waits for them, and re-layouts  1.35 us

profile of v8, /device:TPU:225, one launch (start us, length us, event | category | flops | bytes accessed | tf_op | source)
XLA Modules:
  0.0 47.4 jit_solution(16163990379855982939)
XLA Ops:
  0.0 0.0 copy-start.3
  0.0 0.7 %copy-done.3 = s32[2,64]{1,0:T(2,128)S(1)} copy-done((s32[2,64]{1,0:T(2,128)S(1)}, s32[2,64]{1,0:T(2,128)}, u32[]{:S(2)}) %copy-start.3) | copy-done | bytes 536
  0.7 0.0 copy-start
  0.7 0.0 copy-start.1
  0.7 0.0 copy-start.2
  0.7 46.0 %packed.1 = (bf16[256,256]{1,0:T(8,128)(2,1)S(1)}, f32[1,128]{1,0:T(1,128)S(1)}) custom-call(s32[2,64]{1,0:T(2,128)S(1)} %copy-done.3, bf16[16,16,256]{2,1,0:T(8,128)(2,1)} %bitcast.9, bf16[16,16,256]{2,1,0:T(8,128)(2,1)} %bitcast.11, bf16[16,16,256]{2,1,0:T(8,128)(2,1)} %bitcast.13), custom_call_target="tpu_custom_call" | custom-call | tf_op jit(solution)/shard_map/packed/pallas_call | solution.py:566
  46.7 0.0 copy-done
  46.8 0.0 copy-done.1
  46.8 0.0 copy-done.2
  46.8 0.7 %copy.10 = bf16[256,256]{1,0:T(8,128)(2,1)} copy(bf16[256,256]{1,0:T(8,128)(2,1)S(1)} %get-tuple-element.26) | data formatting | bytes 262144
  (1 shorter events, 0.0 us)
Async XLA Ops:
  0.0 0.7 %copy-start.3 = (s32[2,64]{1,0:T(2,128)S(1)}, s32[2,64]{1,0:T(2,128)}, u32[]{:S(2)}) copy-start(s32[2,64]{1,0:T(2,128)} %partner_hbm.1) | copy-start | bytes 1540
  0.7 46.1 %copy-start = (bf16[256,256]{1,0:T(8,128)(2,1)S(1)}, bf16[256,256]{1,0:T(8,128)(2,1)}, u32[]{:S(2)}) copy-start(bf16[256,256]{1,0:T(8,128)(2,1)} %param.6) | copy-start | bytes 393220
  0.7 46.1 %copy-start.1 = (bf16[256,256]{1,0:T(8,128)(2,1)S(1)}, bf16[256,256]{1,0:T(8,128)(2,1)}, u32[]{:S(2)}) copy-start(bf16[256,256]{1,0:T(8,128)(2,1)} %param.7) | copy-start | bytes 393220
  0.7 46.1 %copy-start.2 = (bf16[256,256]{1,0:T(8,128)(2,1)S(1)}, bf16[256,256]{1,0:T(8,128)(2,1)}, u32[]{:S(2)}) copy-start(bf16[256,256]{1,0:T(8,128)(2,1)} %param.8) | copy-start | bytes 393220

commit v9 on v8

--- a/solution.py
+++ b/solution.py
@@ -259,7 +259,7 @@
             pack[h][k] = own[h][jnp.clip(block - base, 0, plane - 1)]
             return d + 1
 
-        lax.fori_loop(0, slots, take, 0)
+        lax.fori_loop(0, slots, take, 0, unroll=2)
 
     def give_back(h):
         exchange(h, 0).wait_recv()
@@ -273,7 +273,7 @@
             pick[h, j] = jnp.where(near, mine, theirs)
             return taken + jnp.where(near, 0, 1)
 
-        lax.fori_loop(0, plane, choose, 0)
+        lax.fori_loop(0, plane, choose, 0, unroll=4)
         each_peer(
             lambda j, d: remote(
                 pick.at[h, j], part.at[h, i], back_send.at[h], back_recv.at[h], d

time: 47.6 us -> 47.3 us (level)
  no operation moved by 1% of the time
where the time goes in v9:
time: 47.3 us; the launch traced here: 47.2 us
  Pallas kernels  45.8 us (97%)
  local copies, waits for them, and re-layouts  1.35 us (3%)
    pallas_call x1, Pallas kernels, call(): pl.pallas_call(functools.partial(sparse_attention_kernel, plane, groups,...  45.8 us
    unnamed x9, local copies, waits for them, and re-layouts  1.35 us

profile of v9, /device:TPU:225, one launch (start us, length us, event | category | flops | bytes accessed | tf_op | source)
XLA Modules:
  0.0 47.2 jit_solution(2584737525436633115)
XLA Ops:
  0.0 0.0 copy-start.3
  0.0 0.7 %copy-done.3 = s32[2,64]{1,0:T(2,128)S(1)} copy-done((s32[2,64]{1,0:T(2,128)S(1)}, s32[2,64]{1,0:T(2,128)}, u32[]{:S(2)}) %copy-start.3) | copy-done | bytes 536
  0.7 0.0 copy-start
  0.7 0.0 copy-start.1
  0.7 0.0 copy-start.2
  0.7 45.8 %packed.1 = (bf16[256,256]{1,0:T(8,128)(2,1)S(1)}, f32[1,128]{1,0:T(1,128)S(1)}) custom-call(s32[2,64]{1,0:T(2,128)S(1)} %copy-done.3, bf16[16,16,256]{2,1,0:T(8,128)(2,1)} %bitcast.9, bf16[16,16,256]{2,1,0:T(8,128)(2,1)} %bitcast.11, bf16[16,16,256]{2,1,0:T(8,128)(2,1)} %bitcast.13), custom_call_target="tpu_custom_call" | custom-call | tf_op jit(solution)/shard_map/packed/pallas_call | solution.py:566
  46.5 0.0 copy-done
  46.5 0.0 copy-done.1
  46.5 0.0 copy-done.2
  46.5 0.7 %copy.10 = bf16[256,256]{1,0:T(8,128)(2,1)} copy(bf16[256,256]{1,0:T(8,128)(2,1)S(1)} %get-tuple-element.26) | data formatting | bytes 262144
  (1 shorter events, 0.0 us)
Async XLA Ops:
  0.0 0.7 %copy-start.3 = (s32[2,64]{1,0:T(2,128)S(1)}, s32[2,64]{1,0:T(2,128)}, u32[]{:S(2)}) copy-start(s32[2,64]{1,0:T(2,128)} %partner_hbm.1) | copy-start | bytes 1540
  0.7 45.8 %copy-start = (bf16[256,256]{1,0:T(8,128)(2,1)S(1)}, bf16[256,256]{1,0:T(8,128)(2,1)}, u32[]{:S(2)}) copy-start(bf16[256,256]{1,0:T(8,128)(2,1)} %param.6) | copy-start | bytes 393220
  0.7 45.8 %copy-start.1 = (bf16[256,256]{1,0:T(8,128)(2,1)S(1)}, bf16[256,256]{1,0:T(8,128)(2,1)}, u32[]{:S(2)}) copy-start(bf16[256,256]{1,0:T(8,128)(2,1)} %param.7) | copy-start | bytes 393220
  0.7 45.8 %copy-start.2 = (bf16[256,256]{1,0:T(8,128)(2,1)S(1)}, bf16[256,256]{1,0:T(8,128)(2,1)}, u32[]{:S(2)}) copy-start(bf16[256,256]{1,0:T(8,128)(2,1)} %param.8) | copy-start | bytes 393220

commit v10 on v9

--- a/solution.py
+++ b/solution.py
@@ -492,9 +492,9 @@
         followers = sum(jnp.where(g == leader, 1, 0) for _, leader in turns)
         pl.semaphore_wait(barrier, plane - 1 + groups + followers)
         signal(ready, mirror)
+        spread(0)
         for og in range(groups):
             to_column(mirror, og)
-        spread(0)
         spread(1)
         tables()
         spread_done(0)

time: 47.3 us -> 47.8 us (1.011)
  no operation moved by 1% of the time
where the time goes in v10:
time: 47.8 us; the launch traced here: 47.6 us
  Pallas kernels  46.2 us (97%)
  local copies, waits for them, and re-layouts  1.35 us (3%)
    pallas_call x1, Pallas kernels, call(): pl.pallas_call(functools.partial(sparse_attention_kernel, plane, groups,...  46.2 us
    unnamed x9, local copies, waits for them, and re-layouts  1.35 us

profile of v10, /device:TPU:225, one launch (start us, length us, event | category | flops | bytes accessed | tf_op | source)
XLA Modules:
  0.0 47.6 jit_solution(2803283563420542452)
XLA Ops:
  0.0 0.0 copy-start.3
  0.0 0.7 %copy-done.3 = s32[2,64]{1,0:T(2,128)S(1)} copy-done((s32[2,64]{1,0:T(2,128)S(1)}, s32[2,64]{1,0:T(2,128)}, u32[]{:S(2)}) %copy-start.3) | copy-done | bytes 536
  0.7 0.0 copy-start
  0.7 0.0 copy-start.1
  0.7 0.0 copy-start.2
  0.7 46.2 %packed.1 = (bf16[256,256]{1,0:T(8,128)(2,1)S(1)}, f32[1,128]{1,0:T(1,128)S(1)}) custom-call(s32[2,64]{1,0:T(2,128)S(1)} %copy-done.3, bf16[16,16,256]{2,1,0:T(8,128)(2,1)} %bitcast.9, bf16[16,16,256]{2,1,0:T(8,128)(2,1)} %bitcast.11, bf16[16,16,256]{2,1,0:T(8,128)(2,1)} %bitcast.13), custom_call_target="tpu_custom_call" | custom-call | tf_op jit(solution)/shard_map/packed/pallas_call | solution.py:566
  46.9 0.0 copy-done
  46.9 0.0 copy-done.1
  46.9 0.0 copy-done.2
  47.0 0.7 %copy.10 = bf16[256,256]{1,0:T(8,128)(2,1)} copy(bf16[256,256]{1,0:T(8,128)(2,1)S(1)} %get-tuple-element.26) | data formatting | bytes 262144
  (1 shorter events, 0.0 us)
Async XLA Ops:
  0.0 0.7 %copy-start.3 = (s32[2,64]{1,0:T(2,128)S(1)}, s32[2,64]{1,0:T(2,128)}, u32[]{:S(2)}) copy-start(s32[2,64]{1,0:T(2,128)} %partner_hbm.1) | copy-start | bytes 1540
  0.7 46.2 %copy-start = (bf16[256,256]{1,0:T(8,128)(2,1)S(1)}, bf16[256,256]{1,0:T(8,128)(2,1)}, u32[]{:S(2)}) copy-start(bf16[256,256]{1,0:T(8,128)(2,1)} %param.6) | copy-start | bytes 393220
  0.7 46.2 %copy-start.1 = (bf16[256,256]{1,0:T(8,128)(2,1)S(1)}, bf16[256,256]{1,0:T(8,128)(2,1)}, u32[]{:S(2)}) copy-start(bf16[256,256]{1,0:T(8,128)(2,1)} %param.7) | copy-start | bytes 393220
  0.7 46.3 %copy-start.2 = (bf16[256,256]{1,0:T(8,128)(2,1)S(1)}, bf16[256,256]{1,0:T(8,128)(2,1)}, u32[]{:S(2)}) copy-start(bf16[256,256]{1,0:T(8,128)(2,1)} %param.8) | copy-start | bytes 393220

commit v11 on v9

--- a/solution.py
+++ b/solution.py
@@ -200,13 +200,13 @@
                 after[h, d] = jnp.where(here(partner[h, across + d]), d, after[h, d + 1])
                 return c
 
-            lax.fori_loop(0, plane, link, 0)
+            lax.fori_loop(0, plane, link, 0, unroll=4)
 
     def count(h):
         def add(d, n):
             return n + jnp.where(here(partner[h, across + d]), 1, 0)
 
-        return lax.fori_loop(0, plane, add, 0)
+        return lax.fori_loop(0, plane, add, 0, unroll=4)
 
     def to_column(seq, head):
         rows = pl.ds(2 * g, 2)
@@ -273,7 +273,7 @@
             pick[h, j] = jnp.where(near, mine, theirs)
             return taken + jnp.where(near, 0, 1)
 
-        lax.fori_loop(0, plane, choose, 0, unroll=4)
+        lax.fori_loop(0, plane, choose, 0, unroll=8)
         each_peer(
             lambda j, d: remote(
                 pick.at[h, j], part.at[h, i], back_send.at[h], back_recv.at[h], d
@@ -392,7 +392,7 @@
                 x = x - (top + jnp.log(jnp.sum(jnp.exp(x - top), axis=along, keepdims=True)))
             return x
 
-        x = lax.fori_loop(0, SINK_ITERS, sweep, x)
+        x = lax.fori_loop(0, SINK_ITERS, sweep, x, unroll=2)
         row = lax.broadcasted_iota(jnp.int32, x.shape, 0)
         col = lax.broadcasted_iota(jnp.int32, x.shape, 1)
         for which, block in ((0, s), (1, mirror)):
@@ -440,7 +440,7 @@
 
             return c
 
-        lax.fori_loop(0, slices, to_owner, 0)
+        lax.fori_loop(0, slices, to_owner, 0, unroll=2)
         spread_done(1)
         fill(1)
 

time: 47.3 us -> 47.3 us (level)
  no operation moved by 1% of the time
where the time goes in v11:
time: 47.3 us; the launch traced here: 47.2 us
  Pallas kernels  45.7 us (97%)
  local copies, waits for them, and re-layouts  1.35 us (3%)
    pallas_call x1, Pallas kernels, call(): pl.pallas_call(functools.partial(sparse_attention_kernel, plane, groups,...  45.7 us
    unnamed x9, local copies, waits for them, and re-layouts  1.35 us

profile of v11, /device:TPU:225, one launch (start us, length us, event | category | flops | bytes accessed | tf_op | source)
XLA Modules:
  0.0 47.2 jit_solution(1370596734479293922)
XLA Ops:
  0.0 0.0 copy-start.3
  0.0 0.7 %copy-done.3 = s32[2,64]{1,0:T(2,128)S(1)} copy-done((s32[2,64]{1,0:T(2,128)S(1)}, s32[2,64]{1,0:T(2,128)}, u32[]{:S(2)}) %copy-start.3) | copy-done | bytes 536
  0.7 0.0 copy-start
  0.7 0.0 copy-start.1
  0.7 0.0 copy-start.2
  0.7 45.7 %packed.1 = (bf16[256,256]{1,0:T(8,128)(2,1)S(1)}, f32[1,128]{1,0:T(1,128)S(1)}) custom-call(s32[2,64]{1,0:T(2,128)S(1)} %copy-done.3, bf16[16,16,256]{2,1,0:T(8,128)(2,1)} %bitcast.9, bf16[16,16,256]{2,1,0:T(8,128)(2,1)} %bitcast.11, bf16[16,16,256]{2,1,0:T(8,128)(2,1)} %bitcast.13), custom_call_target="tpu_custom_call" | custom-call | tf_op jit(solution)/shard_map/packed/pallas_call | solution.py:566
  46.5 0.0 copy-done
  46.5 0.0 copy-done.1
  46.5 0.0 copy-done.2
  46.5 0.7 %copy.10 = bf16[256,256]{1,0:T(8,128)(2,1)} copy(bf16[256,256]{1,0:T(8,128)(2,1)S(1)} %get-tuple-element.26) | data formatting | bytes 262144
  (1 shorter events, 0.0 us)
Async XLA Ops:
  0.0 0.7 %copy-start.3 = (s32[2,64]{1,0:T(2,128)S(1)}, s32[2,64]{1,0:T(2,128)}, u32[]{:S(2)}) copy-start(s32[2,64]{1,0:T(2,128)} %partner_hbm.1) | copy-start | bytes 1540
  0.7 45.8 %copy-start = (bf16[256,256]{1,0:T(8,128)(2,1)S(1)}, bf16[256,256]{1,0:T(8,128)(2,1)}, u32[]{:S(2)}) copy-start(bf16[256,256]{1,0:T(8,128)(2,1)} %param.6) | copy-start | bytes 393220
  0.7 45.8 %copy-start.1 = (bf16[256,256]{1,0:T(8,128)(2,1)S(1)}, bf16[256,256]{1,0:T(8,128)(2,1)}, u32[]{:S(2)}) copy-start(bf16[256,256]{1,0:T(8,128)(2,1)} %param.7) | copy-start | bytes 393220
  0.7 45.8 %copy-start.2 = (bf16[256,256]{1,0:T(8,128)(2,1)S(1)}, bf16[256,256]{1,0:T(8,128)(2,1)}, u32[]{:S(2)}) copy-start(bf16[256,256]{1,0:T(8,128)(2,1)} %param.8) | copy-start | bytes 393220
